TPU v7x, 32 devices: a whole 2x2x4 slice. The times are simulated.
32 devices in a mesh: row: 8 (over y, x, core), col: 4 (over z).
Axes of the slice: x: 2, y: 2, z: 4, core: 2. Of those that a mesh axis runs over, the one named last changes fastest.
Arguments:
- pair: bfloat16 [384, 384, 128], P('row', 'col'), may hold values from -6 to 6
- token_mask: int32 [384], replicated, may hold values from 0 to 1, as said below
- gain: float32 [2, 128], replicated, may hold values from 0.25 to 1.75
- w_proj: bfloat16 [2, 128, 512], replicated, may hold values from -3 to 3
- w_bias: bfloat16 [2, 128, 4], replicated, may hold values from -0.5 to 0.5
- w_out: bfloat16 [2, 128, 128], replicated, may hold values from -0.5 to 0.5
Outputs:
- updated: bfloat16 [384, 384, 128], P('row', 'col')
Inputs may be any that keep to these rules, and one draw needn't show every extreme that they name: `token_mask`: the tokens form 4 chains of 96 positions each; in each chain the first L positions are 1 and the rest 0, with 48 <= L < 96.
All inputs are finite; a program needn't handle non-finite values.
Results may differ from a plain program's by a relative error of at most 0.03.
The roundings to bfloat16 on the way count: a program that leaves them out, or rounds other values in their place, can miss the bound.
Values may be sent and summed in bfloat16 or wider, within the bound.
A program may use at most 128 MiB of HBM per device.

v0:
```python
import math

import jax
import jax.numpy as jnp
from jax import lax
from jax.sharding import PartitionSpec as P

HEADS = 4
HEAD_DIM = 32


def normalize(tile, gain):
    values = tile.astype(jnp.float32)
    average = jnp.mean(values, axis=-1, keepdims=True)
    centred = values - average
    variance = jnp.mean(centred * centred, axis=-1, keepdims=True)
    return (centred * lax.rsqrt(variance + 1e-05) * gain).astype(jnp.bfloat16)


def project(normed, w_proj, w_bias):
    row_count, col_count, channels = normed.shape
    inner = HEADS * HEAD_DIM
    flattened = normed.reshape(row_count * col_count, channels)
    projected = jnp.dot(flattened, w_proj, preferred_element_type=jnp.float32)
    queries = (projected[:, :inner] / jnp.sqrt(jnp.float32(HEAD_DIM))).astype(jnp.bfloat16)
    queries = queries.reshape(row_count, col_count, HEADS, HEAD_DIM)
    key_part = (
        projected[:, inner : 2 * inner].astype(jnp.bfloat16).reshape(row_count, col_count, inner)
    )
    value_part = (
        projected[:, 2 * inner : 3 * inner]
        .astype(jnp.bfloat16)
        .reshape(row_count, col_count, inner)
    )
    gate_part = jax.nn.sigmoid(projected[:, 3 * inner :])
    bias_part = jnp.dot(flattened, w_bias, preferred_element_type=jnp.float32).astype(jnp.bfloat16)
    return (
        queries,
        key_part,
        value_part,
        gate_part,
        bias_part.reshape(row_count, col_count, HEADS),
    )


def keys_from_pairs(normed_piece, w_proj):
    inner = HEADS * HEAD_DIM
    lead = normed_piece.shape[:2]
    flattened = normed_piece.reshape(lead[0] * lead[1], normed_piece.shape[2])
    projected = jnp.dot(flattened, w_proj[:, inner : 3 * inner], preferred_element_type=jnp.float32)
    key_piece = projected[:, :inner].astype(jnp.bfloat16).reshape(lead + (inner,))
    value_piece = projected[:, inner:].astype(jnp.bfloat16).reshape(lead + (inner,))
    return (key_piece, value_piece)


def accumulate(carried, scores, value_piece, form):
    running_max, running_sum, running_acc = carried
    new_max = jnp.maximum(running_max, jnp.max(scores, axis=-1))
    factor = jnp.exp(running_max - new_max)
    weights = jnp.exp(scores - new_max[..., None])
    running_sum = running_sum * factor + jnp.sum(weights, axis=-1)
    product = jnp.einsum(
        form, weights.astype(jnp.bfloat16), value_piece, preferred_element_type=jnp.float32
    )
    return (new_max, running_sum, running_acc * factor[..., None] + product)


def attend_ending(carried, key_piece, value_piece, offset, queries, bias_end, token_mask):
    count = key_piece.shape[0]
    col_count = queries.shape[1]
    key_four = key_piece.reshape(count, col_count, HEADS, HEAD_DIM)
    value_four = value_piece.reshape(count, col_count, HEADS, HEAD_DIM)
    scores = jnp.einsum("ijhd,kjhd->ijhk", queries, key_four, preferred_element_type=jnp.float32)
    bias_slice = lax.dynamic_slice_in_dim(bias_end, offset, count, 0)
    scores = scores + jnp.transpose(bias_slice, (1, 2, 0)).astype(jnp.float32)[:, None]
    live = lax.dynamic_slice_in_dim(token_mask, offset, count, 0)
    scores = jnp.where(live > 0, scores, -1000000000.0)
    return accumulate(carried, scores, value_four, "ijhk,kjhd->ijhd")


def attend_starting(carried, key_piece, value_piece, offset, queries, bias_start, token_mask):
    count = key_piece.shape[1]
    row_count = queries.shape[0]
    key_four = key_piece.reshape(row_count, count, HEADS, HEAD_DIM)
    value_four = value_piece.reshape(row_count, count, HEADS, HEAD_DIM)
    scores = jnp.einsum("ijhd,ikhd->ijhk", queries, key_four, preferred_element_type=jnp.float32)
    bias_slice = lax.dynamic_slice_in_dim(bias_start, offset, count, 1)
    scores = scores + jnp.transpose(bias_slice, (0, 2, 1)).astype(jnp.float32)[None]
    live = lax.dynamic_slice_in_dim(token_mask, offset, count, 0)
    scores = jnp.where(live > 0, scores, -1000000000.0)
    return accumulate(carried, scores, value_four, "ijhk,ikhd->ijhd")


def fold_blocks(carried, pieces, along, convert, attend):
    count = pieces[0].shape[along]
    width = math.gcd(count, 128)

    def one_block(index, carry):
        start = index * width
        blocks = tuple((lax.dynamic_slice_in_dim(piece, start, width, along) for piece in pieces))
        key_block, value_block = convert(blocks)
        return attend(carry, key_block, value_block, start)

    return lax.fori_loop(0, count // width, one_block, carried)


def select_bias(bias_part, row_count, col_count, ending):
    bias_rowwise = lax.all_gather(bias_part, "row", axis=0, tiled=True)
    full_bias = lax.all_gather(bias_rowwise, "col", axis=1, tiled=True)
    if ending:
        return lax.dynamic_slice_in_dim(full_bias, lax.axis_index("row") * row_count, row_count, 1)
    return lax.dynamic_slice_in_dim(full_bias, lax.axis_index("col") * col_count, col_count, 0)


def run_pass(tile, token_mask, gain, w_proj, w_bias, w_out, ending):
    row_count, col_count, channels = tile.shape
    normed = normalize(tile, gain)
    queries, key_part, value_part, gate_part, bias_part = project(normed, w_proj, w_bias)
    bias_local = select_bias(bias_part, row_count, col_count, ending)
    start_max = jnp.full((row_count, col_count, HEADS), -1e30, jnp.float32)
    start_sum = jnp.zeros((row_count, col_count, HEADS), jnp.float32)
    start_acc = jnp.zeros((row_count, col_count, HEADS, HEAD_DIM), jnp.float32)
    initial = (start_max, start_sum, start_acc)

    def project_pairs(blocks):
        return keys_from_pairs(blocks[0], w_proj)

    if ending:

        def ending_step(carry, key_block, value_block, position):
            return attend_ending(
                carry, key_block, value_block, position, queries, bias_local, token_mask
            )

        def fold_pairs(carried, received, offset):
            return fold_blocks(carried, (received,), 0, project_pairs, ending_step)

        result = fold_pairs(
            initial, lax.all_gather(normed, "row", axis=0, tiled=True), jnp.int32(0)
        )
    else:

        def starting_step(carry, key_block, value_block, position):
            return attend_starting(
                carry, key_block, value_block, position, queries, bias_local, token_mask
            )

        def fold_pairs(carried, received, offset):
            return fold_blocks(carried, (received,), 1, project_pairs, starting_step)

        result = fold_pairs(
            initial, lax.all_gather(normed, "col", axis=1, tiled=True), jnp.int32(0)
        )
    final_max, final_sum, final_acc = result
    attended = final_acc / final_sum[..., None]
    gated = (gate_part * attended.reshape(row_count * col_count, HEADS * HEAD_DIM)).astype(
        jnp.bfloat16
    )
    update = jnp.dot(gated, w_out, preferred_element_type=jnp.float32)
    return (tile.astype(jnp.float32) + update.reshape(row_count, col_count, channels)).astype(
        jnp.bfloat16
    )


def local(pair, token_mask, gain, w_proj, w_bias, w_out):
    first = run_pass(pair, token_mask, gain[0], w_proj[0], w_bias[0], w_out[0], True)
    return run_pass(first, token_mask, gain[1], w_proj[1], w_bias[1], w_out[1], False)


def solution(mesh):
    return jax.shard_map(
        local,
        mesh=mesh,
        in_specs=(P("row", "col", None), P(), P(), P(), P(), P()),
        out_specs=P("row", "col", None),
        check_vma=False,
    )
```

profile of v0, /device:TPU:0, one launch (start us, length us, event | category | flops | bytes accessed | tf_op | source)
XLA Modules:
  0.0 606.2 jit_solution(17036669407147317621)
XLA Ops:
  13.7 11.1 %all_gather.19 = bf16[384,96,4]{1,2,0:T(4,128)(2,1)S(1)} all-gather(bf16[48,96,4]{1,2,0:T(4,128)(2,1)S(1)} %copy.62), channel_id=1, replica_groups=mesh['row'=8,'col'=4] {'row'}, dimensions={0}, use_global_device_ids=true | all-gather | bytes 331776 | tf_op jit(solution)/shard_map/all_gather | solution.py:108
  41.4 15.1 %all-gather.7.cloned.1.call-done = bf16[384,384,4]{0,2,1:T(4,128)(2,1)} async-done(((bf16[384,96,4]{0,2,1:T(4,128)(2,1)}), bf16[384,384,4]{0,2,1:T(4,128)(2,1)}) %all-gather.7.cloned.1.call-update) | async-done | bytes 1179664 | tf_op jit(solution)/shard_map/all_gather | solution.py:109
  58.1 58.2 %all-gather.5.cloned.1.call-done = bf16[384,96,128]{2,1,0:T(8,128)(2,1)} async-done(((bf16[48,96,128]{2,1,0:T(8,128)(2,1)}), bf16[384,96,128]{2,1,0:T(8,128)(2,1)}) %all-gather.5.cloned.1.call-update) | async-done | bytes 9437200 | tf_op jit(solution)/shard_map/all_gather | solution.py:139
  116.3 207.7 %while.36 = (s32[]{:T(128)}, f32[48,96,4]{0,2,1:T(4,128)}, f32[48,96,4]{0,2,1:T(4,128)}, f32[48,96,4,32]{0,3,2,1:T(8,128)}, s32[384]{0:T(512)S(1)}, /*index=5*/b...) while((s32[]{:T(128)}, f32[48,96,4]{0,2,1:T(4,128)}, ...), condition=%wide.region_5.6_spmd.clone, body=%wide.region_2.5_spmd.clone.sunk | while | flops 1138280576 | bytes 109233432 | solution.py:104
  132.6 6.1 %copy.98 = bf16[128,96,4,32]{0,3,2,1:T(8,128)(2,1)S(1)} copy(bf16[128,96,4,32]{1,0,3,2:T(8,128)(2,1)} %reshape.122) | data formatting | bytes 6291456 | tf_op jit(solution)/shard_map/while/body/eval_jaxpr/reshape;while/body/eval_jaxpr/reshape | solution.py:71
  139.7 10.1 %fusion.107 = (f32[48,96,4]{0,2,1:T(4,128)}, f32[96,4,128,48]{2,3,1,0:T(8,128)}) fusion(f32[48,4,128]{2,0,1:T(8,128)S(1)} %convert_bitcast_fusion.4, pred[128]{0:T(512)(128)(4,1)S(1)} %dynamic-slice_compare_fusion.4, bf16[128,96,4,32]{0,3,2,1:T(8,128)(2,1)S(1)} %copy.98, bf16[48,96,4,32]{0,3,2,1:T(8,128)(2,1)} %get-tuple-element.672), kind=kOutput, calls=%fused_computation.6.clone.1 | convolution fusion | flops 158054400 | bytes 13934720 | tf_op jit(solution)/shard_map/while/body/eval_jaxpr/ijhd,kjhd->ijhk/dot_general | solution.py:73
  150.8 8.3 %fusion.108 = f32[48,96,4]{0,2,1:T(4,128)S(1)} fusion(f32[96,4,128,48]{2,3,1,0:T(8,128)} %get-tuple-element.620, f32[48,96,4]{0,2,1:T(4,128)S(1)} %select_maximum_fusion.4, f32[48,4,128]{2,0,1:T(8,128)S(1)} %convert_bitcast_fusion.4, pred[128]{0:T(512)(128)(4,1)S(1)} %dynamic-slice_compare_fusion.4), kind=kLoop, calls=%fused_computation.5.clone.1 | loop fusion | flops 9418752 | bytes 9683072 | tf_op jit(solution)/shard_map/while/body/eval_jaxpr/reduce_sum | solution.py:61
  169.1 6.1 %copy.100 = bf16[128,96,4,32]{0,3,2,1:T(8,128)(2,1)S(1)} copy(bf16[128,96,4,32]{1,0,3,2:T(8,128)(2,1)} %reshape.123) | data formatting | bytes 6291456 | tf_op jit(solution)/shard_map/while/body/eval_jaxpr/reshape;while/body/eval_jaxpr/reshape | solution.py:72
  175.2 8.7 %bitcast_add_fusion.6 = f32[48,96,4,32]{0,3,2,1:T(8,128)} fusion(f32[48,96,4,32]{0,3,2,1:T(8,128)} %get-tuple-element.655, f32[48,96,4]{0,2,1:T(4,128)} %get-tuple-element.622, pred[]{:T(512)S(6)} %compare.6, bf16[128,96,4,32]{0,3,2,1:T(8,128)(2,1)S(1)} %copy.100, f32[96,4,128,48]{2,3,1,0:T(8,128)} %get-tuple-element.620, ...), kind=kOutput, calls=%fused_computation.7.clone.1 | convolution fusion | flops 162201600 | bytes 17547392 | tf_op jit(solution)/shard_map/while/body/eval_jaxpr/ijhk,kjhd->ijhd/dot_general | solution.py:62
  200.7 6.1 %copy.98 = bf16[128,96,4,32]{0,3,2,1:T(8,128)(2,1)S(1)} copy(bf16[128,96,4,32]{1,0,3,2:T(8,128)(2,1)} %reshape.122) | data formatting | bytes 6291456 | tf_op jit(solution)/shard_map/while/body/eval_jaxpr/reshape;while/body/eval_jaxpr/reshape | solution.py:71
  207.8 10.1 %fusion.107 = (f32[48,96,4]{0,2,1:T(4,128)}, f32[96,4,128,48]{2,3,1,0:T(8,128)}) fusion(f32[48,4,128]{2,0,1:T(8,128)S(1)} %convert_bitcast_fusion.4, pred[128]{0:T(512)(128)(4,1)S(1)} %dynamic-slice_compare_fusion.4, bf16[128,96,4,32]{0,3,2,1:T(8,128)(2,1)S(1)} %copy.98, bf16[48,96,4,32]{0,3,2,1:T(8,128)(2,1)} %get-tuple-element.672), kind=kOutput, calls=%fused_computation.6.clone.1 | convolution fusion | flops 158054400 | bytes 13934720 | tf_op jit(solution)/shard_map/while/body/eval_jaxpr/ijhd,kjhd->ijhk/dot_general | solution.py:73
  219.0 8.3 %fusion.108 = f32[48,96,4]{0,2,1:T(4,128)S(1)} fusion(f32[96,4,128,48]{2,3,1,0:T(8,128)} %get-tuple-element.620, f32[48,96,4]{0,2,1:T(4,128)S(1)} %select_maximum_fusion.4, f32[48,4,128]{2,0,1:T(8,128)S(1)} %convert_bitcast_fusion.4, pred[128]{0:T(512)(128)(4,1)S(1)} %dynamic-slice_compare_fusion.4), kind=kLoop, calls=%fused_computation.5.clone.1 | loop fusion | flops 9418752 | bytes 9683072 | tf_op jit(solution)/shard_map/while/body/eval_jaxpr/reduce_sum | solution.py:61
  237.3 6.1 %copy.100 = bf16[128,96,4,32]{0,3,2,1:T(8,128)(2,1)S(1)} copy(bf16[128,96,4,32]{1,0,3,2:T(8,128)(2,1)} %reshape.123) | data formatting | bytes 6291456 | tf_op jit(solution)/shard_map/while/body/eval_jaxpr/reshape;while/body/eval_jaxpr/reshape | solution.py:72
  243.4 10.1 %bitcast_add_fusion.6 = f32[48,96,4,32]{0,3,2,1:T(8,128)} fusion(f32[48,96,4,32]{0,3,2,1:T(8,128)} %get-tuple-element.655, f32[48,96,4]{0,2,1:T(4,128)} %get-tuple-element.622, pred[]{:T(512)S(6)} %compare.6, bf16[128,96,4,32]{0,3,2,1:T(8,128)(2,1)S(1)} %copy.100, f32[96,4,128,48]{2,3,1,0:T(8,128)} %get-tuple-element.620, ...), kind=kOutput, calls=%fused_computation.7.clone.1 | convolution fusion | flops 162201600 | bytes 17547392 | tf_op jit(solution)/shard_map/while/body/eval_jaxpr/ijhk,kjhd->ijhd/dot_general | solution.py:62
  270.3 6.1 %copy.98 = bf16[128,96,4,32]{0,3,2,1:T(8,128)(2,1)S(1)} copy(bf16[128,96,4,32]{1,0,3,2:T(8,128)(2,1)} %reshape.122) | data formatting | bytes 6291456 | tf_op jit(solution)/shard_map/while/body/eval_jaxpr/reshape;while/body/eval_jaxpr/reshape | solution.py:71
  277.4 10.1 %fusion.107 = (f32[48,96,4]{0,2,1:T(4,128)}, f32[96,4,128,48]{2,3,1,0:T(8,128)}) fusion(f32[48,4,128]{2,0,1:T(8,128)S(1)} %convert_bitcast_fusion.4, pred[128]{0:T(512)(128)(4,1)S(1)} %dynamic-slice_compare_fusion.4, bf16[128,96,4,32]{0,3,2,1:T(8,128)(2,1)S(1)} %copy.98, bf16[48,96,4,32]{0,3,2,1:T(8,128)(2,1)} %get-tuple-element.672), kind=kOutput, calls=%fused_computation.6.clone.1 | convolution fusion | flops 158054400 | bytes 13934720 | tf_op jit(solution)/shard_map/while/body/eval_jaxpr/ijhd,kjhd->ijhk/dot_general | solution.py:73
  288.6 8.3 %fusion.108 = f32[48,96,4]{0,2,1:T(4,128)S(1)} fusion(f32[96,4,128,48]{2,3,1,0:T(8,128)} %get-tuple-element.620, f32[48,96,4]{0,2,1:T(4,128)S(1)} %select_maximum_fusion.4, f32[48,4,128]{2,0,1:T(8,128)S(1)} %convert_bitcast_fusion.4, pred[128]{0:T(512)(128)(4,1)S(1)} %dynamic-slice_compare_fusion.4), kind=kLoop, calls=%fused_computation.5.clone.1 | loop fusion | flops 9418752 | bytes 9683072 | tf_op jit(solution)/shard_map/while/body/eval_jaxpr/reduce_sum | solution.py:61
  306.9 6.1 %copy.100 = bf16[128,96,4,32]{0,3,2,1:T(8,128)(2,1)S(1)} copy(bf16[128,96,4,32]{1,0,3,2:T(8,128)(2,1)} %reshape.123) | data formatting | bytes 6291456 | tf_op jit(solution)/shard_map/while/body/eval_jaxpr/reshape;while/body/eval_jaxpr/reshape | solution.py:72
  313.0 10.1 %bitcast_add_fusion.6 = f32[48,96,4,32]{0,3,2,1:T(8,128)} fusion(f32[48,96,4,32]{0,3,2,1:T(8,128)} %get-tuple-element.655, f32[48,96,4]{0,2,1:T(4,128)} %get-tuple-element.622, pred[]{:T(512)S(6)} %compare.6, bf16[128,96,4,32]{0,3,2,1:T(8,128)(2,1)S(1)} %copy.100, f32[96,4,128,48]{2,3,1,0:T(8,128)} %get-tuple-element.620, ...), kind=kOutput, calls=%fused_computation.7.clone.1 | convolution fusion | flops 162201600 | bytes 17547392 | tf_op jit(solution)/shard_map/while/body/eval_jaxpr/ijhk,kjhd->ijhd/dot_general | solution.py:62
  324.0 6.9 %broadcast_divide_fusion = f32[48,96,4,32]{0,3,2,1:T(8,128)} fusion(f32[48,96,4,32]{0,3,2,1:T(8,128)} %get-tuple-element.315, f32[48,96,4]{0,2,1:T(4,128)} %get-tuple-element.316), kind=kLoop, calls=%fused_computation.58 | loop fusion | flops 589824 | bytes 4792320 | tf_op jit(solution)/shard_map/div | solution.py:155
  330.9 5.4 copy.66
  348.3 9.5 %all_gather.22 = bf16[384,96,4]{1,2,0:T(4,128)(2,1)S(1)} all-gather(bf16[48,96,4]{1,2,0:T(4,128)(2,1)S(1)} %copy.69), channel_id=1, replica_groups=mesh['row'=8,'col'=4] {'row'}, dimensions={0}, use_global_device_ids=true | all-gather | bytes 331776 | tf_op jit(solution)/shard_map/all_gather | solution.py:108
  370.0 19.2 %all-gather.11.cloned.1.call-done = bf16[384,384,4]{0,2,1:T(4,128)(2,1)} async-done(((bf16[384,96,4]{0,2,1:T(4,128)(2,1)}), bf16[384,384,4]{0,2,1:T(4,128)(2,1)}) %all-gather.11.cloned.1.call-update) | async-done | bytes 1179664 | tf_op jit(solution)/shard_map/all_gather | solution.py:109
  391.6 87.7 %all-gather.9.cloned.1.call-done = bf16[48,384,128]{2,1,0:T(8,128)(2,1)} async-done(((bf16[48,96,128]{2,1,0:T(8,128)(2,1)}), bf16[48,384,128]{2,1,0:T(8,128)(2,1)}) %all-gather.9.cloned.1.call-update) | async-done | bytes 4718608 | tf_op jit(solution)/shard_map/all_gather | solution.py:152
  479.3 107.2 %while.37 = (s32[]{:T(128)}, f32[48,96,4]{1,2,0:T(4,128)S(1)}, f32[48,96,4]{1,2,0:T(4,128)}, f32[48,96,4,32]{1,3,2,0:T(8,128)}, s32[384]{0:T(512)S(1)}, /*index=...) while((s32[]{:T(128)}, f32[48,96,4]{1,2,0:T(4,128)S(1)}, ...), condition=%wide.region_11.12_spmd.clone, body=%wide.region_8.11_spmd.clone.sunk | while | flops 734079104 | bytes 90703208 | solution.py:104
  492.6 8.7 %fusion.117 = f32[48,96,4]{1,2,0:T(4,128)S(1)} fusion(f32[48,4,128,96]{2,3,1,0:T(8,128)} %get-tuple-element.635, f32[48,96,4]{1,2,0:T(4,128)S(1)} %select_maximum_fusion.5, f32[96,4,128]{2,0,1:T(8,128)S(1)} %convert_bitcast_fusion.5, pred[128]{0:T(512)(128)(4,1)S(1)} %dynamic-slice_compare_fusion.5), kind=kLoop, calls=%fused_computation.28.clone.1 | loop fusion | flops 9418752 | bytes 9781376 | tf_op jit(solution)/shard_map/while/body/eval_jaxpr/reduce_sum | solution.py:61
  504.7 8.0 %bitcast_add_fusion.7 = f32[48,96,4,32]{1,3,2,0:T(8,128)S(1)} fusion(f32[48,96,4,32]{1,3,2,0:T(8,128)S(1)} %copy-done, f32[48,4,128,96]{2,3,1,0:T(8,128)} %get-tuple-element.635, f32[48,96,4]{1,2,0:T(4,128)S(1)} %select_maximum_fusion.5, f32[96,4,128]{2,0,1:T(8,128)S(1)} %convert_bitcast_fusion.5, ...), kind=kOutput, calls=%fused_computation.36.clone.1 | convolution fusion | flops 162201600 | bytes 16072833 | tf_op jit(solution)/shard_map/while/body/eval_jaxpr/ijhk,ikhd->ijhd/dot_general | solution.py:62
  522.3 5.4 fusion.116
  527.8 8.7 %fusion.117 = f32[48,96,4]{1,2,0:T(4,128)S(1)} fusion(f32[48,4,128,96]{2,3,1,0:T(8,128)} %get-tuple-element.635, f32[48,96,4]{1,2,0:T(4,128)S(1)} %select_maximum_fusion.5, f32[96,4,128]{2,0,1:T(8,128)S(1)} %convert_bitcast_fusion.5, pred[128]{0:T(512)(128)(4,1)S(1)} %dynamic-slice_compare_fusion.5), kind=kLoop, calls=%fused_computation.28.clone.1 | loop fusion | flops 9418752 | bytes 9781376 | tf_op jit(solution)/shard_map/while/body/eval_jaxpr/reduce_sum | solution.py:61
  540.8 8.0 %bitcast_add_fusion.7 = f32[48,96,4,32]{1,3,2,0:T(8,128)S(1)} fusion(f32[48,96,4,32]{1,3,2,0:T(8,128)S(1)} %copy-done, f32[48,4,128,96]{2,3,1,0:T(8,128)} %get-tuple-element.635, f32[48,96,4]{1,2,0:T(4,128)S(1)} %select_maximum_fusion.5, f32[96,4,128]{2,0,1:T(8,128)S(1)} %convert_bitcast_fusion.5, ...), kind=kOutput, calls=%fused_computation.36.clone.1 | convolution fusion | flops 162201600 | bytes 16072833 | tf_op jit(solution)/shard_map/while/body/eval_jaxpr/ijhk,ikhd->ijhd/dot_general | solution.py:62
  563.8 8.7 %fusion.117 = f32[48,96,4]{1,2,0:T(4,128)S(1)} fusion(f32[48,4,128,96]{2,3,1,0:T(8,128)} %get-tuple-element.635, f32[48,96,4]{1,2,0:T(4,128)S(1)} %select_maximum_fusion.5, f32[96,4,128]{2,0,1:T(8,128)S(1)} %convert_bitcast_fusion.5, pred[128]{0:T(512)(128)(4,1)S(1)} %dynamic-slice_compare_fusion.5), kind=kLoop, calls=%fused_computation.28.clone.1 | loop fusion | flops 9418752 | bytes 9781376 | tf_op jit(solution)/shard_map/while/body/eval_jaxpr/reduce_sum | solution.py:61
  576.8 8.0 %bitcast_add_fusion.7 = f32[48,96,4,32]{1,3,2,0:T(8,128)S(1)} fusion(f32[48,96,4,32]{1,3,2,0:T(8,128)S(1)} %copy-done, f32[48,4,128,96]{2,3,1,0:T(8,128)} %get-tuple-element.635, f32[48,96,4]{1,2,0:T(4,128)S(1)} %select_maximum_fusion.5, f32[96,4,128]{2,0,1:T(8,128)S(1)} %convert_bitcast_fusion.5, ...), kind=kOutput, calls=%fused_computation.36.clone.1 | convolution fusion | flops 162201600 | bytes 16072833 | tf_op jit(solution)/shard_map/while/body/eval_jaxpr/ijhk,ikhd->ijhd/dot_general | solution.py:62
  (221 shorter events, 201.9 us)
Async XLA Ops:
  6.5 5.1 copy-start.10
  6.5 4.6 copy-start.24
  6.5 6.6 %copy-start.21 = (bf16[2,128,4]{1,2,0:T(4,128)(2,1)S(1)}, bf16[2,128,4]{1,2,0:T(4,128)(2,1)}, u32[]{:S(2)}) copy-start(bf16[2,128,4]{1,2,0:T(4,128)(2,1)} %param.14) | copy-start | bytes 6148
  6.5 49.9 %all-gather.7.cloned.1.call-start = ((), (), s32[]{:S(2)}) async-start(), calls=%async_computation.1 | async-start | bytes 1474560 | tf_op jit(solution)/shard_map/all_gather | solution.py:109
  13.1 12.7 %copy-start.5 = (bf16[48,96,128]{2,1,0:T(8,128)(2,1)}, bf16[48,96,128]{2,1,0:T(8,128)(2,1)S(1)}, u32[]{:S(2)}) copy-start(bf16[48,96,128]{2,1,0:T(8,128)(2,1)S(1)} %fusion.42) | copy-start | bytes 3538948
  13.1 13.5 %copy-start.17 = (bf16[2,128,512]{2,1,0:T(8,128)(2,1)S(1)}, bf16[2,128,512]{2,1,0:T(8,128)(2,1)}, u32[]{:S(2)}) copy-start(bf16[2,128,512]{2,1,0:T(8,128)(2,1)} %param.13) | copy-start | bytes 786436
  25.8 90.6 %all-gather.5.cloned.1.call-start = ((), (), s32[]{:S(2)}) async-start(), calls=%async_computation | async-start | bytes 10616832 | tf_op jit(solution)/shard_map/all_gather | solution.py:139
  26.5 362.7 %all-gather.11.cloned.1.call-start = ((), (), s32[]{:S(2)}) async-start(), calls=%async_computation.3 | async-start | bytes 1474560 | tf_op jit(solution)/shard_map/all_gather | solution.py:109
  29.3 3.7 copy-start.3
  35.4 80.9 %copy-start.25 = (s32[384]{0:T(512)S(1)}, s32[384]{0:T(512)}, u32[]{:S(2)}) copy-start(s32[384]{0:T(512)} %param.11) | copy-start | bytes 4612
  150.8 8.3 %copy-start.7 = (f32[48,96,4]{0,2,1:T(4,128)S(1)}, f32[48,96,4]{0,2,1:T(4,128)}, u32[]{:S(2)}) copy-start(f32[48,96,4]{0,2,1:T(4,128)} %get-tuple-element.653) | copy-start | bytes 221188 | tf_op jit(solution)/shard_map/while
  150.8 8.3 %copy-start.13 = (f32[48,96,4]{0,2,1:T(4,128)S(1)}, f32[48,96,4]{0,2,1:T(4,128)}, u32[]{:S(2)}) copy-start(f32[48,96,4]{0,2,1:T(4,128)} %get-tuple-element.654) | copy-start | bytes 221188 | tf_op jit(solution)/shard_map/while
  219.0 8.3 %copy-start.7 = (f32[48,96,4]{0,2,1:T(4,128)S(1)}, f32[48,96,4]{0,2,1:T(4,128)}, u32[]{:S(2)}) copy-start(f32[48,96,4]{0,2,1:T(4,128)} %get-tuple-element.653) | copy-start | bytes 221188 | tf_op jit(solution)/shard_map/while
  219.0 8.3 %copy-start.13 = (f32[48,96,4]{0,2,1:T(4,128)S(1)}, f32[48,96,4]{0,2,1:T(4,128)}, u32[]{:S(2)}) copy-start(f32[48,96,4]{0,2,1:T(4,128)} %get-tuple-element.654) | copy-start | bytes 221188 | tf_op jit(solution)/shard_map/while
  288.6 8.3 %copy-start.7 = (f32[48,96,4]{0,2,1:T(4,128)S(1)}, f32[48,96,4]{0,2,1:T(4,128)}, u32[]{:S(2)}) copy-start(f32[48,96,4]{0,2,1:T(4,128)} %get-tuple-element.653) | copy-start | bytes 221188 | tf_op jit(solution)/shard_map/while
  288.6 8.3 %copy-start.13 = (f32[48,96,4]{0,2,1:T(4,128)S(1)}, f32[48,96,4]{0,2,1:T(4,128)}, u32[]{:S(2)}) copy-start(f32[48,96,4]{0,2,1:T(4,128)} %get-tuple-element.654) | copy-start | bytes 221188 | tf_op jit(solution)/shard_map/while
  341.0 2.4 copy-start.11
  341.0 2.4 copy-start.19
  343.4 2.8 copy-start.23
  344.5 3.2 copy-start.22
  347.7 11.2 %copy-start.6 = (bf16[48,96,128]{2,1,0:T(8,128)(2,1)}, bf16[48,96,128]{2,1,0:T(8,128)(2,1)S(1)}, u32[]{:S(2)}) copy-start(bf16[48,96,128]{2,1,0:T(8,128)(2,1)S(1)} %fusion.39) | copy-start | bytes 3538948
  347.7 11.7 %copy-start.18 = (bf16[2,128,512]{2,1,0:T(8,128)(2,1)S(1)}, bf16[2,128,512]{2,1,0:T(8,128)(2,1)}, u32[]{:S(2)}) copy-start(bf16[2,128,512]{2,1,0:T(8,128)(2,1)} %param.13) | copy-start | bytes 786436
  358.8 120.5 %all-gather.9.cloned.1.call-start = ((), (), s32[]{:S(2)}) async-start(), calls=%async_computation.2 | async-start | bytes 5898240 | tf_op jit(solution)/shard_map/all_gather | solution.py:152
  362.1 3.7 copy-start.4
  479.3 13.3 %copy-start.12 = (f32[48,96,4]{1,2,0:T(4,128)}, f32[48,96,4]{1,2,0:T(4,128)S(1)}, u32[]{:S(2)}) copy-start(f32[48,96,4]{1,2,0:T(4,128)S(1)} %get-tuple-element.692) | copy-start | bytes 221188 | tf_op jit(solution)/shard_map/while
  492.6 8.7 %copy-start.15 = (f32[48,96,4]{1,2,0:T(4,128)S(1)}, f32[48,96,4]{1,2,0:T(4,128)}, u32[]{:S(2)}) copy-start(f32[48,96,4]{1,2,0:T(4,128)} %get-tuple-element.693) | copy-start | bytes 221188 | tf_op jit(solution)/shard_map/while
  514.4 13.3 %copy-start.12 = (f32[48,96,4]{1,2,0:T(4,128)}, f32[48,96,4]{1,2,0:T(4,128)S(1)}, u32[]{:S(2)}) copy-start(f32[48,96,4]{1,2,0:T(4,128)S(1)} %get-tuple-element.692) | copy-start | bytes 221188 | tf_op jit(solution)/shard_map/while
  527.8 8.7 %copy-start.15 = (f32[48,96,4]{1,2,0:T(4,128)S(1)}, f32[48,96,4]{1,2,0:T(4,128)}, u32[]{:S(2)}) copy-start(f32[48,96,4]{1,2,0:T(4,128)} %get-tuple-element.693) | copy-start | bytes 221188 | tf_op jit(solution)/shard_map/while
  550.5 13.3 %copy-start.12 = (f32[48,96,4]{1,2,0:T(4,128)}, f32[48,96,4]{1,2,0:T(4,128)S(1)}, u32[]{:S(2)}) copy-start(f32[48,96,4]{1,2,0:T(4,128)S(1)} %get-tuple-element.692) | copy-start | bytes 221188 | tf_op jit(solution)/shard_map/while
  563.8 8.7 %copy-start.15 = (f32[48,96,4]{1,2,0:T(4,128)S(1)}, f32[48,96,4]{1,2,0:T(4,128)}, u32[]{:S(2)}) copy-start(f32[48,96,4]{1,2,0:T(4,128)} %get-tuple-element.693) | copy-start | bytes 221188 | tf_op jit(solution)/shard_map/while
  595.4 2.4 copy-start.9
  595.4 2.4 copy-start.20
  (16 other events, 20.8 us)
Sparse Core Ops, SparseCore 0:
  25.9 30.5 all-gather.6
  58.4 57.9 all-gather.4
  358.9 30.2 all-gather.10
  390.6 88.6 all-gather.8
where the time goes:
time: 615 us; the launch traced here: 606 us
  local copies, waits for them, and re-layouts  181 us (29%)
  waiting for transfers between devices  181 us (29%)
  matrix products  121 us (20%)
  other arithmetic  86.8 us (14%)
  blocking collectives  20.6 us (3%)
  between operations  14 us (2%)
    all_gather x1, waiting for transfers between devices, run_pass(): lax.all_gather(normed, 'col', axis=1, tiled=True)  87.7 us
    all_gather x1, waiting for transfers between devices, run_pass(): lax.all_gather(normed, 'row', axis=0, tiled=True)  58.2 us
    dot_general x6, matrix products, accumulate(): jnp.einsum(form, weights.astype(jnp.bfloat16), value_piece, preferred_ele...  52.8 us
    reduce_sum x6, other arithmetic, accumulate(): running_sum = running_sum * factor + jnp.sum(weights, axis=-1)  51.1 us
    all_gather x2, waiting for transfers between devices, select_bias(): full_bias = lax.all_gather(bias_rowwise, 'col', axis=1, tiled=True)  34.3 us
    reshape x6, local copies, waits for them, and re-layouts, attend_ending(): value_four = value_piece.reshape(count, col_count, HEADS, HEAD_DIM)  33.9 us
    reshape x6, local copies, waits for them, and re-layouts, attend_ending(): key_four = key_piece.reshape(count, col_count, HEADS, HEAD_DIM)  33.8 us
    dot_general x3, matrix products, attend_ending(): jnp.einsum('ijhd,kjhd->ijhk', queries, key_four, preferred_element_type=j...  30.3 us
  transfers between devices with their start and end apart: 4, of which 4 were waited for; matrix products, arithmetic and copies ran while one was open for 4% of the time, Pallas kernels for 0%

commit v1 on v0

v1 whole, which is shorter than its diff:
```python
import functools
import math

import jax
import jax.numpy as jnp
from jax import lax
from jax.experimental import pallas as pl
from jax.experimental.pallas import tpu as pltpu
from jax.sharding import PartitionSpec as P

HEADS = 4
HEAD_DIM = 32
INNER = HEADS * HEAD_DIM
LOG2E = 1.4426950408889634
NT = (((1,), (1,)), ((), ()))
TN = (((0,), (0,)), ((), ()))


def normalize(tile, gain):
    values = tile.astype(jnp.float32)
    average = jnp.mean(values, axis=-1, keepdims=True)
    centred = values - average
    variance = jnp.mean(centred * centred, axis=-1, keepdims=True)
    return (centred * lax.rsqrt(variance + 1e-05) * gain).astype(jnp.bfloat16)


def attend(x, bias_ref, gain_ref, w_qvg_ref, w_k_ref, w_out_ref):
    count = x.shape[0]
    normed = normalize(x, gain_ref[...])
    qvg = lax.dot_general(w_qvg_ref[...], normed, NT, preferred_element_type=jnp.float32)
    keys = jnp.dot(normed, w_k_ref[...], preferred_element_type=jnp.float32).astype(jnp.bfloat16)
    queries = (qvg[:INNER] * (LOG2E / math.sqrt(HEAD_DIM))).astype(jnp.bfloat16)
    values = qvg[INNER : 2 * INNER].astype(jnp.bfloat16)
    gate = jax.nn.sigmoid(qvg[2 * INNER :])
    ones = jnp.ones((16, count), jnp.bfloat16)
    pieces = []
    for head in range(HEADS):
        low, high = head * HEAD_DIM, (head + 1) * HEAD_DIM
        parts = [queries[low:high]]
        if head:
            parts.insert(0, jnp.zeros((low, count), jnp.bfloat16))
        if head < HEADS - 1:
            parts.append(jnp.zeros((INNER - high, count), jnp.bfloat16))
        padded = jnp.concatenate(parts, axis=0)
        scores = jnp.dot(keys, padded, preferred_element_type=jnp.float32) + bias_ref[head]
        highest = jnp.max(scores, axis=0, keepdims=True)
        weights = jnp.exp2(scores - highest).astype(jnp.bfloat16)
        extended = jnp.concatenate([values[low:high], ones], axis=0)
        mixed = jnp.dot(extended, weights, preferred_element_type=jnp.float32)
        pieces.append(mixed[:HEAD_DIM] * (1.0 / mixed[HEAD_DIM : HEAD_DIM + 1]))
    gated = (gate * jnp.concatenate(pieces, axis=0)).astype(jnp.bfloat16)
    update = lax.dot_general(gated, w_out_ref[...], TN, preferred_element_type=jnp.float32)
    return (x.astype(jnp.float32) + update).astype(jnp.bfloat16)


def attention_kernel(x_ref, bias_ref, gain_ref, w_qvg_ref, w_k_ref, w_out_ref, out_ref):
    out_ref[0] = attend(x_ref[0], bias_ref, gain_ref, w_qvg_ref, w_k_ref, w_out_ref)


def split_weights(w_proj):
    w_turned = jnp.transpose(w_proj)
    w_qvg = jnp.concatenate([w_turned[:INNER], w_turned[2 * INNER :]], axis=0)
    return w_qvg, w_proj[:, INNER : 2 * INNER]


def attention(x, bias, gain, w_proj, w_out):
    rows, count, channels = x.shape
    w_qvg, w_k = split_weights(w_proj)
    whole = lambda *shape: pl.BlockSpec(shape, lambda i: (0,) * len(shape))
    return pl.pallas_call(
        attention_kernel,
        out_shape=jax.ShapeDtypeStruct(x.shape, jnp.bfloat16),
        grid=(rows,),
        in_specs=[
            pl.BlockSpec((1, count, channels), lambda i: (i, 0, 0)),
            whole(HEADS, count, count),
            whole(1, channels),
            whole(3 * INNER, channels),
            whole(channels, INNER),
            whole(INNER, channels),
        ],
        out_specs=pl.BlockSpec((1, count, channels), lambda i: (i, 0, 0)),
    )(x, bias, gain[None], w_qvg, w_k, w_out)


def meet(peers):
    barrier = pltpu.get_barrier_semaphore()
    for peer in peers:
        pl.semaphore_signal(barrier, inc=1, device_id=peer, device_id_type=pl.DeviceIdType.MESH)
    pl.semaphore_wait(barrier, len(peers))


def remote(source, target, send_sem, recv_sem, peer):
    return pltpu.make_async_remote_copy(
        src_ref=source,
        dst_ref=target,
        send_sem=send_sem,
        recv_sem=recv_sem,
        device_id=peer,
        device_id_type=pl.DeviceIdType.MESH,
    )


def exchange_kernel(size, shifts, piece_of, place_of, x_ref, out_ref, send_sems, recv_sems, own_sem):
    rows, cols = size
    row, col = lax.axis_index("row"), lax.axis_index("col")
    to = [(lax.rem(row + dr, rows), lax.rem(col + dc, cols)) for dr, dc in shifts]
    meet(to)
    copies = []
    for at, peer in enumerate(to):
        copy = remote(
            piece_of(x_ref, *peer), place_of(out_ref, row, col), send_sems.at[at], recv_sems.at[at], peer
        )
        copy.start()
        copies.append(copy)
    own = pltpu.make_async_copy(piece_of(x_ref, row, col), place_of(out_ref, row, col), own_sem)
    own.start()
    own.wait()
    for at, (dr, dc) in enumerate(shifts):
        source = (lax.rem(row + rows - dr, rows), lax.rem(col + cols - dc, cols))
        remote(
            piece_of(x_ref, row, col), place_of(out_ref, *source), send_sems.at[at], recv_sems.at[at], to[at]
        ).wait_recv()
    for copy in copies:
        copy.wait_send()


def exchange(x, out_shape, size, axes, piece_of, place_of, collective_id):
    shifts = shifts_of(size, axes)
    return pl.pallas_call(
        functools.partial(exchange_kernel, size, shifts, piece_of, place_of),
        out_shape=jax.ShapeDtypeStruct(out_shape, x.dtype),
        in_specs=[pl.BlockSpec(memory_space=pltpu.VMEM)],
        out_specs=pl.BlockSpec(memory_space=pltpu.VMEM),
        scratch_shapes=[
            pltpu.SemaphoreType.DMA((len(shifts),)),
            pltpu.SemaphoreType.DMA((len(shifts),)),
            pltpu.SemaphoreType.DMA,
        ],
        compiler_params=pltpu.CompilerParams(collective_id=collective_id, has_side_effects=True),
    )(x)


def gather_peers(size):
    rows, cols = size
    row, col = lax.axis_index("row"), lax.axis_index("col")
    in_col = [(row, lax.rem(col + d, cols)) for d in range(1, cols)]
    in_row = [(lax.rem(row + 2 * d, rows), col) for d in range(1, rows // 2)]
    partner = (row // 2 * 2 + 1 - lax.rem(row, 2), col)
    return in_col, in_row, partner


def gather_stages(size, part_ref, full_ref, send_sems, recv_sems, own_sem):
    rows, cols = size
    row, col = lax.axis_index("row"), lax.axis_index("col")
    half, core = row // 2, lax.rem(row, 2)
    in_col, in_row, partner = gather_peers(size)
    sent = []

    def send(source, target, at, peer):
        copy = remote(source, target, send_sems.at[at], recv_sems.at[at], peer)
        copy.start()
        sent.append(copy)

    def arrive(target, at, peer):
        remote(target, target, send_sems.at[at], recv_sems.at[at], peer).wait_recv()

    mine = full_ref.at[core, half, col]
    for at, peer in enumerate(in_col):
        send(part_ref, mine, at, peer)
    own = pltpu.make_async_copy(part_ref, mine, own_sem)
    own.start()
    own.wait()
    for at, peer in enumerate(in_col):
        arrive(full_ref.at[core, half, lax.rem(col + cols - at - 1, cols)], at, peer)
    base = len(in_col)
    for at, peer in enumerate(in_row):
        send(full_ref.at[core, half], full_ref.at[core, half], base + at, peer)
    halves = rows // 2
    for at, peer in enumerate(in_row):
        arrive(full_ref.at[core, lax.rem(half + halves - at - 1, halves)], base + at, peer)
    base += len(in_row)
    send(full_ref.at[core], full_ref.at[core], base, partner)
    arrive(full_ref.at[1 - core], base, partner)
    for copy in sent:
        copy.wait_send()


def gather_kernel(size, part_ref, full_ref, send_sems, recv_sems, own_sem):
    in_col, in_row, partner = gather_peers(size)
    meet(in_col + in_row + [partner])
    gather_stages(size, part_ref, full_ref, send_sems, recv_sems, own_sem)


def fused_kernel(
    size, shifts, piece_of, place_of, bias_too, x_ref, bias_ref, gain_ref, w_qvg_ref, w_k_ref, w_out_ref, *rest
):
    if bias_too:
        next_gain_ref, w_bias_ref, out_ref, full_ref, stage, send_sems, recv_sems, own_sem = rest[:8]
        part, gather_send, gather_recv, gather_own = rest[8:]
    else:
        out_ref, stage, send_sems, recv_sems, own_sem = rest
    width = x_ref.shape[0]
    rows, cols = size
    row, col = lax.axis_index("row"), lax.axis_index("col")
    to = [(lax.rem(row + dr, rows), lax.rem(col + dc, cols)) for dr, dc in shifts]
    meet(to)

    def push(at):
        one = pl.ds(at, 1)
        for index, peer in enumerate(to):
            remote(
                piece_of(stage, one, *peer),
                place_of(out_ref, one, row, col),
                send_sems.at[index],
                recv_sems.at[index],
                peer,
            ).start()
        pltpu.make_async_copy(piece_of(stage, one, row, col), place_of(out_ref, one, row, col), own_sem).start()

    def step(at, carry):
        @pl.when(at > 0)
        def _():
            push(at - 1)

        result = attend(x_ref[at], bias_ref, gain_ref, w_qvg_ref, w_k_ref, w_out_ref)
        stage[at] = result.reshape(stage.shape[1:])
        if bias_too:
            turned = lax.dot_general(
                w_bias_ref[...], normalize(result, next_gain_ref[...]), NT, preferred_element_type=jnp.float32
            )
            part[at] = turned[:HEADS].astype(jnp.bfloat16)
        return carry

    lax.fori_loop(0, width, step, 0)
    push(width - 1)
    if bias_too:
        gather_stages(size, part, full_ref, gather_send, gather_recv, gather_own)
    every = pl.ds(0, width)
    mine = piece_of(stage, every, row, col)
    pltpu.make_async_copy(mine, place_of(out_ref, every, row, col), own_sem).wait()
    for index, (dr, dc) in enumerate(shifts):
        source = (lax.rem(row + rows - dr, rows), lax.rem(col + cols - dc, cols))
        remote(
            mine, place_of(out_ref, every, *source), send_sems.at[index], recv_sems.at[index], to[index]
        ).wait_recv()
    for index, peer in enumerate(to):
        remote(
            piece_of(stage, every, *peer), place_of(out_ref, every, row, col), send_sems.at[index], recv_sems.at[index], peer
        ).wait_send()


def shifts_of(size, axes):
    return [
        (dr, dc)
        for dc in (range(size[1]) if "col" in axes else (0,))
        for dr in (range(size[0]) if "row" in axes else (0,))
        if dr or dc
    ]


def fused(x, bias, gain, w_proj, w_out, out_shape, stage_shape, size, axes, piece_of, place_of, collective_id, following=None):
    shifts = shifts_of(size, axes)
    operands = [x, bias, gain[None], *split_weights(w_proj), w_out]
    outs = [jax.ShapeDtypeStruct(out_shape, x.dtype)]
    scratch = [
        pltpu.VMEM(stage_shape, x.dtype),
        pltpu.SemaphoreType.DMA((len(shifts),)),
        pltpu.SemaphoreType.DMA((len(shifts),)),
        pltpu.SemaphoreType.DMA,
    ]
    if following is not None:
        next_gain, w_bias = following
        operands += [next_gain[None], jnp.pad(jnp.transpose(w_bias), ((0, 16 - HEADS), (0, 0)))]
        part_shape = (x.shape[0], HEADS, x.shape[1])
        outs.append(jax.ShapeDtypeStruct((2, size[0] // 2, size[1]) + part_shape, x.dtype))
        count = size[1] - 1 + size[0] // 2
        scratch += [
            pltpu.VMEM(part_shape, x.dtype),
            pltpu.SemaphoreType.DMA((count,)),
            pltpu.SemaphoreType.DMA((count,)),
            pltpu.SemaphoreType.DMA,
        ]
    return pl.pallas_call(
        functools.partial(fused_kernel, size, shifts, piece_of, place_of, following is not None),
        out_shape=outs,
        in_specs=[pl.BlockSpec(memory_space=pltpu.VMEM)] * len(operands),
        out_specs=[pl.BlockSpec(memory_space=pltpu.VMEM)] * len(outs),
        scratch_shapes=scratch,
        compiler_params=pltpu.CompilerParams(collective_id=collective_id, has_side_effects=True),
    )(*operands)


def gather(part, size, collective_id):
    count = size[1] - 1 + size[0] // 2 - 1 + 1
    return pl.pallas_call(
        functools.partial(gather_kernel, size),
        out_shape=jax.ShapeDtypeStruct((2, size[0] // 2, size[1]) + part.shape, part.dtype),
        in_specs=[pl.BlockSpec(memory_space=pltpu.VMEM)],
        out_specs=pl.BlockSpec(memory_space=pltpu.VMEM),
        scratch_shapes=[
            pltpu.SemaphoreType.DMA((count,)),
            pltpu.SemaphoreType.DMA((count,)),
            pltpu.SemaphoreType.DMA,
        ],
        compiler_params=pltpu.CompilerParams(collective_id=collective_id, has_side_effects=True),
    )(part)


def gather_bias(x, token_mask, gain, w_bias, size, ending):
    rows, count, channels = x.shape
    normed = normalize(x, gain)
    part = jnp.einsum("ikc,ch->ihk", normed, w_bias, preferred_element_type=jnp.float32)
    full = gather(part.astype(jnp.bfloat16), size, 0 if ending else 1)
    order = (4, 5, 2, 1, 0, 3) if ending else (4, 5, 1, 0, 2, 3)
    turned = jnp.transpose(full, order).reshape(HEADS, count, count).astype(jnp.float32) * LOG2E
    return jnp.where(token_mask[None, :, None] > 0, turned, -1000000000.0)


def swap(x, size):
    width, count, channels = x.shape
    rows, cols = size
    if width % 2:
        x = lax.all_to_all(x, "row", 1, 0, tiled=True)
        return lax.all_to_all(jnp.transpose(x, (1, 0, 2)), "col", 0, 1, tiled=True)
    pairs = width // 2
    moved = exchange(
        x.reshape(width, count // 2, 2, channels),
        (cols, rows, width, pairs, 2, channels),
        size,
        ("row", "col"),
        lambda ref, r, c: ref.at[:, pl.ds((r * cols + c) * pairs, pairs)],
        lambda ref, r, c: ref.at[c, r],
        3,
    )
    return jnp.transpose(moved.reshape(count, width, channels), (1, 0, 2))


def local(pair, token_mask, gain, w_proj, w_bias, w_out, size):
    rows, cols = size
    deep, wide, channels = pair.shape
    width, count = wide // rows, deep * rows
    flipped = jnp.transpose(pair, (1, 0, 2))
    x = exchange(
        flipped,
        (width, count, channels),
        size,
        ("row",),
        lambda ref, r, c: ref.at[pl.ds(r * width, width)],
        lambda ref, r, c: ref.at[:, pl.ds(pl.multiple_of(r * deep, deep), deep)],
        2,
    )
    bias = gather_bias(x, token_mask, gain[0], w_bias[0], size, True)
    if width % 2:
        x = attention(x, bias, gain[0], w_proj[0], w_out[0])
        x = swap(x, size)
        bias = gather_bias(x, token_mask, gain[1], w_bias[1], size, False)
    else:
        pairs = width // 2
        moved, full = fused(
            x,
            bias,
            gain[0],
            w_proj[0],
            w_out[0],
            (cols, rows, width, pairs, 2, channels),
            (width, count // 2, 2, channels),
            size,
            ("row", "col"),
            lambda ref, at, r, c: ref.at[at, pl.ds((r * cols + c) * pairs, pairs)],
            lambda ref, at, r, c: ref.at[c, r, at],
            3,
            (gain[1], w_bias[1]),
        )
        x = jnp.transpose(moved.reshape(count, width, channels), (1, 0, 2))
        turned = jnp.transpose(full, (4, 2, 1, 0, 3, 5)).reshape(HEADS, count, count)
        bias = jnp.where(token_mask[None, :, None] > 0, turned.astype(jnp.float32) * LOG2E, -1000000000.0)
    return fused(
        x,
        bias,
        gain[1],
        w_proj[1],
        w_out[1],
        pair.shape,
        x.shape,
        size,
        ("col",),
        lambda ref, at, r, c: ref.at[at, pl.ds(pl.multiple_of(c * wide, wide), wide)],
        lambda ref, at, r, c: ref.at[pl.ds(c * width + at.start, at.size)],
        4,
    )[0]


def solution(mesh):
    size = (mesh.shape["row"], mesh.shape["col"])
    return jax.shard_map(
        functools.partial(local, size=size),
        mesh=mesh,
        in_specs=(P("row", "col", None), P(), P(), P(), P(), P()),
        out_specs=P("row", "col", None),
        check_vma=False,
    )
```

time: 615 us -> 164 us (0.27); the launches traced: 606 us -> 164 us
  waiting for transfers between devices: 181 us -> 0 us
  local copies, waits for them, and re-layouts: 181 us -> 20 us
  Pallas kernels: 0 us -> 128 us
  matrix products: 121 us -> 2.7 us
  other arithmetic: 86.8 us -> 12.7 us
  blocking collectives: 20.6 us -> 0 us
  between operations: 14 us -> 0.17 us
    all_gather x4 -> x0, waiting for transfers between devices: 180 us -> none  [the longest x1 87.7 us: run_pass(): lax.all_gather(normed, 'col', axis=1, tiled=True)]
    pallas_call x0 -> x4, Pallas kernels: none -> 128 us  [the longest x2 89.2 us: fused(): pl.pallas_call(functools.partial(fused_kernel, size, shifts, piece_of, pl...]
    dot_general x24 -> x1, matrix products: 121 us -> 2.7 us  [gather_bias(): jnp.einsum('ikc,ch->ihk', normed, w_bias, preferred_element_type=jnp.floa...]
    reshape x22 -> x2, local copies, waits for them, and re-layouts: 80.4 us -> 4.53 us  [local(): x = jnp.transpose(moved.reshape(count, width, channels), (1, 0, 2))]
    reduce_sum x6 -> x0, other arithmetic: 51.1 us -> none  [accumulate(): running_sum = running_sum * factor + jnp.sum(weights, axis=-1)]
    slice x18 -> x7, local copies, waits for them, and re-layouts: 39.4 us -> 2.56 us  [the longest x1 1.29 us: local(): gain[1]]
    all_gather x2 -> x0, blocking collectives: 20.6 us -> none  [select_bias(): bias_rowwise = lax.all_gather(bias_part, 'row', axis=0, tiled=True)]
    while x66 -> x0, local copies, waits for them, and re-layouts: 17.8 us -> none
  transfers between devices with their start and end apart: 4 -> 0, of which waited for: 4 -> 0; matrix products, arithmetic and copies ran while one was open for 4% -> 0% of each run, Pallas kernels for 0% -> 0%
where the time goes in v1:
time: 164 us
  Pallas kernels  128 us (78%)
  local copies, waits for them, and re-layouts  20 us (12%)
  other arithmetic  12.7 us (8%)
  matrix products  2.7 us (2%)
    pallas_call x2, Pallas kernels, fused(): pl.pallas_call(functools.partial(fused_kernel, size, shifts, piece_of, pl...  89.2 us
    pallas_call x1, Pallas kernels, exchange(): pl.pallas_call(functools.partial(exchange_kernel, size, shifts, piece_of,...  19.5 us
    pallas_call x1, Pallas kernels, gather(): pl.pallas_call(functools.partial(gather_kernel, size), out_shape=jax.Shap...  19.4 us
    reshape x2, local copies, waits for them, and re-layouts, local(): x = jnp.transpose(moved.reshape(count, width, channels), (1, 0, 2))  4.53 us
    unnamed x10, local copies, waits for them, and re-layouts  3.85 us
    select_n x1, other arithmetic, gather_bias(): return jnp.where(token_mask[None, :, None] > 0, turned, -1000000000.0)  3.36 us

profile of v1, /device:TPU:0, one launch (start us, length us, event | category | flops | bytes accessed | tf_op | source)
XLA Modules:
  0.0 163.6 jit_solution(11619454052629790592)
XLA Ops:
  0.0 0.8 broadcast_compare_fusion
  0.8 0.7 slice_bitcast_fusion.6
  1.5 1.3 fusion.15
  2.8 0.6 pad.4.rest_1_
  3.4 1.4 slice_bitcast_fusion.4
  4.8 1.0 slice_bitcast_fusion.1
  5.8 0.6 slice.63.w_k_ref
  6.4 0.6 slice.60.w_k_ref
  7.1 0.8 copy.16.w_qvg_ref
  7.9 0.8 copy.20.w_qvg_ref
  8.6 0.0 copy-done.2
  8.6 1.5 copy.26
  10.1 19.5 %shard_map.64.x_ref = bf16[12,384,128]{2,1,0:T(8,128)(2,1)} custom-call(bf16[96,48,128]{2,1,0:T(8,128)(2,1)} %bitcast.41), custom_call_target="tpu_custom_call" | custom-call | tf_op jit(solution)/shard_map/pallas_call | solution.py:130
  29.7 0.0 copy-start
  29.7 1.7 %convert_reduce_fusion = f32[12,384]{1,0:T(8,128)S(1)} fusion(bf16[12,384,128]{2,1,0:T(8,128)(2,1)} %shard_map.64.x_ref), kind=kLoop, calls=%fused_computation.1 | loop fusion | flops 1175040 | bytes 1198080 | tf_op jit(solution)/shard_map/reduce_sum | solution.py:21
  31.4 2.5 %fusion.2 = f32[12,384]{1,0:T(8,128)S(1)} fusion(bf16[12,384,128]{2,1,0:T(8,128)(2,1)} %shard_map.64.x_ref, f32[12,384]{1,0:T(8,128)S(1)} %broadcast_multiply_fusion), kind=kLoop, calls=%fused_computation.4 | loop fusion | flops 2354688 | bytes 1216512 | tf_op jit(solution)/shard_map/reduce_sum | solution.py:23
  34.0 0.0 copy-done.3
  34.0 0.0 copy-done
  34.0 2.7 %fusion.10.part_ref = bf16[12,4,384]{2,1,0:T(4,128)(2,1)} fusion(bf16[12,384,128]{2,1,0:T(8,128)(2,1)S(1)} %copy-done, f32[128]{0:T(128)S(1)} %get-tuple-element.16, f32[12,384]{1,0:T(8,128)S(1)} %add_rsqrt_fusion, f32[12,384]{1,0:T(8,128)S(1)} %broadcast_multiply_fusion, bf16[2,128,4]{1,2,0:T(4,128)(2,1)S(1)} %copy-done.3), kind=kOutput, calls=%fused_computation.15 | convolution fusion | flops 7686144 | bytes 1267200 | tf_op jit(solution)/shard_map/ikc,ch->ihk/dot_general | solution.py:313
  36.7 19.4 %shard_map.65 = bf16[2,4,4,12,4,384]{5,4,3,2,1,0:T(4,128)(2,1)} custom-call(bf16[12,4,384]{2,1,0:T(4,128)(2,1)} %fusion.10.part_ref), custom_call_target="tpu_custom_call" | custom-call | tf_op jit(solution)/shard_map/pallas_call | solution.py:296
  56.0 1.9 %multiply_bitcast_fusion.1 = f32[4,384,4,4,2,12]{1,0,5,2,3,4:T(4,128)S(1)} fusion(bf16[2,4,4,12,4,384]{5,4,3,2,1,0:T(4,128)(2,1)} %shard_map.65), kind=kLoop, calls=%fused_computation.9 | loop fusion | flops 1179648 | bytes 3538944 | tf_op jit(solution)/shard_map/mul | solution.py:316
  57.9 0.6 copy.14
  58.5 2.6 %copy.15 = f32[4,384,384]{2,1,0:T(8,128)} copy(f32[4,384,384]{1,0,2:T(4,128)S(1)} %bitcast.39) | data formatting | bytes 4718592 | tf_op jit(solution)/shard_map/mul | solution.py:316
  61.1 3.4 %broadcast_select_fusion.bias_ref = f32[4,384,384]{2,1,0:T(8,128)} fusion(f32[4,384,384]{2,1,0:T(8,128)} %copy.15, pred[384]{0:T(512)(128)(4,1)S(1)} %broadcast_compare_fusion), kind=kLoop, calls=%fused_computation.12 | loop fusion | flops 589824 | bytes 4718976 | tf_op jit(solution)/shard_map/jit(_where)/select_n | solution.py:317
  64.5 54.5 %shard_map.66 = (bf16[4,8,12,6,2,128]{5,4,3,2,1,0:T(2,128)(2,1)}, bf16[2,4,4,12,4,384]{5,4,3,2,1,0:T(4,128)(2,1)}) custom-call(bf16[12,384,128]{2,1,0:T(8,128)(2,1)} %shard_map.64.x_ref, f32[4,384,384]{2,1,0:T(8,128)} %broadcast_select_fusion.bias_ref, f32[1,128]{1,0:T(1,128)} %get-tuple-element.17.gain_ref, bf16[384,128]{1,0:T(8,128)(2,1)} %copy.16.w_qvg_ref, ...), custom_call_target="tpu_custom_call" | custom-call | tf_op jit(solution)/shard_map/pallas_call | solution.py:284
  119.0 3.2 %reshape.28 = bf16[384,12,128]{2,1,0:T(8,128)(2,1)S(1)} reshape(bf16[4,8,12,6,2,128]{5,4,3,2,1,0:T(2,128)(2,1)} %get-tuple-element.7) | data formatting | bytes 2359296 | tf_op jit(solution)/shard_map/reshape | solution.py:375
  122.3 1.3 copy.25
  123.6 0.6 multiply_bitcast_fusion
  124.2 0.6 copy.18
  124.8 1.7 %copy_select_fusion.bias_ref = f32[4,384,384]{2,1,0:T(8,128)} fusion(f32[4,384,384]{2,0,1:T(4,128)S(1)} %bitcast.38, pred[384]{0:T(512)(128)(4,1)S(1)} %broadcast_compare_fusion), kind=kLoop, calls=%fused_computation.7 | loop fusion | flops 589824 | bytes 4718976 | tf_op jit(solution)/shard_map/jit(_where)/select_n | solution.py:377
  126.6 34.7 %shard_map.67 = bf16[48,96,128]{2,1,0:T(8,128)(2,1)} custom-call(bf16[12,384,128]{2,1,0:T(8,128)(2,1)} %bitcast.40, f32[4,384,384]{2,1,0:T(8,128)} %copy_select_fusion.bias_ref, f32[1,128]{1,0:T(1,128)} %get-tuple-element.15.rest_0_.gain_ref, bf16[384,128]{1,0:T(8,128)(2,1)} %copy.20.w_qvg_ref, bf16[128,128]{1,0:T(8,128)(2,1)} %slice.63.w_k_ref, ...), custom_call_target="tpu_custom_call" | custom-call | tf_op jit(solution)/shard_map/pallas_call | solution.py:284
  161.3 2.4 %copy.28 = bf16[48,96,128]{2,1,0:T(8,128)(2,1)} copy(bf16[48,96,128]{2,1,0:T(8,128)(2,1)} %shard_map.67) | data formatting | bytes 2359296
  (12 shorter events, 0.1 us)
Async XLA Ops:
  0.0 8.6 %copy-start.2 = (bf16[48,96,128]{2,1,0:T(8,128)(2,1)S(1)}, bf16[48,96,128]{2,1,0:T(8,128)(2,1)}, u32[]{:S(2)}) copy-start(bf16[48,96,128]{2,1,0:T(8,128)(2,1)} %param.6) | copy-start | bytes 3538948
  10.1 23.9 %copy-start.3 = (bf16[2,128,4]{1,2,0:T(4,128)(2,1)S(1)}, bf16[2,128,4]{1,2,0:T(4,128)(2,1)}, u32[]{:S(2)}) copy-start(bf16[2,128,4]{1,2,0:T(4,128)(2,1)} %param.10) | copy-start | bytes 6148
  29.7 4.3 %copy-start = (bf16[12,384,128]{2,1,0:T(8,128)(2,1)S(1)}, bf16[12,384,128]{2,1,0:T(8,128)(2,1)}, u32[]{:S(2)}) copy-start(bf16[12,384,128]{2,1,0:T(8,128)(2,1)} %shard_map.64.x_ref) | copy-start | bytes 3538948
  119.0 4.6 %copy-start.1 = (bf16[2,4,4,12,4,384]{5,4,3,2,1,0:T(4,128)(2,1)S(1)}, bf16[2,4,4,12,4,384]{5,4,3,2,1,0:T(4,128)(2,1)}, u32[]{:S(2)}) copy-start(bf16[2,4,4,12,4,384]{5,4,3,2,1,0:T(4,128)(2,1)} %get-tuple-element.8) | copy-start | bytes 3538948

commit v2 on v1

--- a/solution.py
+++ b/solution.py
@@ -24,14 +24,15 @@
     return (centred * lax.rsqrt(variance + 1e-05) * gain).astype(jnp.bfloat16)
 
 
-def attend(x, bias_ref, gain_ref, w_qvg_ref, w_k_ref, w_out_ref):
+def attend(x, bias_ref, gain, w_turned_ref, w_k, w_out):
     count = x.shape[0]
-    normed = normalize(x, gain_ref[...])
-    qvg = lax.dot_general(w_qvg_ref[...], normed, NT, preferred_element_type=jnp.float32)
-    keys = jnp.dot(normed, w_k_ref[...], preferred_element_type=jnp.float32).astype(jnp.bfloat16)
-    queries = (qvg[:INNER] * (LOG2E / math.sqrt(HEAD_DIM))).astype(jnp.bfloat16)
-    values = qvg[INNER : 2 * INNER].astype(jnp.bfloat16)
-    gate = jax.nn.sigmoid(qvg[2 * INNER :])
+    normed = normalize(x, gain)
+    queries = lax.dot_general(w_turned_ref[:INNER], normed, NT, preferred_element_type=jnp.float32)
+    rest = lax.dot_general(w_turned_ref[2 * INNER :], normed, NT, preferred_element_type=jnp.float32)
+    keys = jnp.dot(normed, w_k, preferred_element_type=jnp.float32).astype(jnp.bfloat16)
+    queries = (queries * (LOG2E / math.sqrt(HEAD_DIM))).astype(jnp.bfloat16)
+    values = rest[:INNER].astype(jnp.bfloat16)
+    gate = jax.nn.sigmoid(rest[INNER:])
     ones = jnp.ones((16, count), jnp.bfloat16)
     pieces = []
     for head in range(HEADS):
@@ -49,23 +50,16 @@
         mixed = jnp.dot(extended, weights, preferred_element_type=jnp.float32)
         pieces.append(mixed[:HEAD_DIM] * (1.0 / mixed[HEAD_DIM : HEAD_DIM + 1]))
     gated = (gate * jnp.concatenate(pieces, axis=0)).astype(jnp.bfloat16)
-    update = lax.dot_general(gated, w_out_ref[...], TN, preferred_element_type=jnp.float32)
+    update = lax.dot_general(gated, w_out, TN, preferred_element_type=jnp.float32)
     return (x.astype(jnp.float32) + update).astype(jnp.bfloat16)
 
 
-def attention_kernel(x_ref, bias_ref, gain_ref, w_qvg_ref, w_k_ref, w_out_ref, out_ref):
-    out_ref[0] = attend(x_ref[0], bias_ref, gain_ref, w_qvg_ref, w_k_ref, w_out_ref)
-
-
-def split_weights(w_proj):
-    w_turned = jnp.transpose(w_proj)
-    w_qvg = jnp.concatenate([w_turned[:INNER], w_turned[2 * INNER :]], axis=0)
-    return w_qvg, w_proj[:, INNER : 2 * INNER]
+def attention_kernel(x_ref, bias_ref, gain_ref, w_turned_ref, w_k_ref, w_out_ref, out_ref):
+    out_ref[0] = attend(x_ref[0], bias_ref, gain_ref[...], w_turned_ref, w_k_ref[...], w_out_ref[...])
 
 
 def attention(x, bias, gain, w_proj, w_out):
     rows, count, channels = x.shape
-    w_qvg, w_k = split_weights(w_proj)
     whole = lambda *shape: pl.BlockSpec(shape, lambda i: (0,) * len(shape))
     return pl.pallas_call(
         attention_kernel,
@@ -75,12 +69,12 @@
             pl.BlockSpec((1, count, channels), lambda i: (i, 0, 0)),
             whole(HEADS, count, count),
             whole(1, channels),
-            whole(3 * INNER, channels),
+            whole(4 * INNER, channels),
             whole(channels, INNER),
             whole(INNER, channels),
         ],
         out_specs=pl.BlockSpec((1, count, channels), lambda i: (i, 0, 0)),
-    )(x, bias, gain[None], w_qvg, w_k, w_out)
+    )(x, bias, gain[None], jnp.transpose(w_proj), w_proj[:, INNER : 2 * INNER], w_out)
 
 
 def meet(peers):
@@ -99,46 +93,6 @@
         device_id=peer,
         device_id_type=pl.DeviceIdType.MESH,
     )
-
-
-def exchange_kernel(size, shifts, piece_of, place_of, x_ref, out_ref, send_sems, recv_sems, own_sem):
-    rows, cols = size
-    row, col = lax.axis_index("row"), lax.axis_index("col")
-    to = [(lax.rem(row + dr, rows), lax.rem(col + dc, cols)) for dr, dc in shifts]
-    meet(to)
-    copies = []
-    for at, peer in enumerate(to):
-        copy = remote(
-            piece_of(x_ref, *peer), place_of(out_ref, row, col), send_sems.at[at], recv_sems.at[at], peer
-        )
-        copy.start()
-        copies.append(copy)
-    own = pltpu.make_async_copy(piece_of(x_ref, row, col), place_of(out_ref, row, col), own_sem)
-    own.start()
-    own.wait()
-    for at, (dr, dc) in enumerate(shifts):
-        source = (lax.rem(row + rows - dr, rows), lax.rem(col + cols - dc, cols))
-        remote(
-            piece_of(x_ref, row, col), place_of(out_ref, *source), send_sems.at[at], recv_sems.at[at], to[at]
-        ).wait_recv()
-    for copy in copies:
-        copy.wait_send()
-
-
-def exchange(x, out_shape, size, axes, piece_of, place_of, collective_id):
-    shifts = shifts_of(size, axes)
-    return pl.pallas_call(
-        functools.partial(exchange_kernel, size, shifts, piece_of, place_of),
-        out_shape=jax.ShapeDtypeStruct(out_shape, x.dtype),
-        in_specs=[pl.BlockSpec(memory_space=pltpu.VMEM)],
-        out_specs=pl.BlockSpec(memory_space=pltpu.VMEM),
-        scratch_shapes=[
-            pltpu.SemaphoreType.DMA((len(shifts),)),
-            pltpu.SemaphoreType.DMA((len(shifts),)),
-            pltpu.SemaphoreType.DMA,
-        ],
-        compiler_params=pltpu.CompilerParams(collective_id=collective_id, has_side_effects=True),
-    )(x)
 
 
 def gather_peers(size):
@@ -193,18 +147,20 @@
 
 
 def fused_kernel(
-    size, shifts, piece_of, place_of, bias_too, x_ref, bias_ref, gain_ref, w_qvg_ref, w_k_ref, w_out_ref, *rest
+    size, shifts, piece_of, place_of, turn, x_ref, bias_ref, gain_ref, w_proj_ref, w_bias_ref, w_out_ref, *rest
 ):
+    bias_too = turn == 0
     if bias_too:
-        next_gain_ref, w_bias_ref, out_ref, full_ref, stage, send_sems, recv_sems, own_sem = rest[:8]
-        part, gather_send, gather_recv, gather_own = rest[8:]
+        out_ref, full_ref, stage, turned_ref, send_sems, recv_sems, own_sem = rest[:7]
+        part, gather_send, gather_recv, gather_own = rest[7:]
     else:
-        out_ref, stage, send_sems, recv_sems, own_sem = rest
+        out_ref, stage, turned_ref, send_sems, recv_sems, own_sem = rest
     width = x_ref.shape[0]
     rows, cols = size
     row, col = lax.axis_index("row"), lax.axis_index("col")
     to = [(lax.rem(row + dr, rows), lax.rem(col + dc, cols)) for dr, dc in shifts]
     meet(to)
+    turned_ref[...] = jnp.transpose(w_proj_ref[turn].astype(jnp.float32)).astype(jnp.bfloat16)
 
     def push(at):
         one = pl.ds(at, 1)
@@ -223,11 +179,18 @@
         def _():
             push(at - 1)
 
-        result = attend(x_ref[at], bias_ref, gain_ref, w_qvg_ref, w_k_ref, w_out_ref)
+        result = attend(
+            x_ref[at],
+            bias_ref,
+            gain_ref[turn : turn + 1],
+            turned_ref,
+            w_proj_ref[turn, :, INNER : 2 * INNER],
+            w_out_ref[turn],
+        )
         stage[at] = result.reshape(stage.shape[1:])
         if bias_too:
             turned = lax.dot_general(
-                w_bias_ref[...], normalize(result, next_gain_ref[...]), NT, preferred_element_type=jnp.float32
+                w_bias_ref[1], normalize(result, gain_ref[1:2]), NT, preferred_element_type=jnp.float32
             )
             part[at] = turned[:HEADS].astype(jnp.bfloat16)
         return carry
@@ -259,19 +222,18 @@
     ]
 
 
-def fused(x, bias, gain, w_proj, w_out, out_shape, stage_shape, size, axes, piece_of, place_of, collective_id, following=None):
+def fused(x, bias, gain, w_proj, w_bias, w_out, turn, out_shape, stage_shape, size, axes, piece_of, place_of, collective_id):
     shifts = shifts_of(size, axes)
-    operands = [x, bias, gain[None], *split_weights(w_proj), w_out]
+    operands = [x, bias, gain, w_proj, w_bias, w_out]
     outs = [jax.ShapeDtypeStruct(out_shape, x.dtype)]
     scratch = [
         pltpu.VMEM(stage_shape, x.dtype),
+        pltpu.VMEM((w_proj.shape[2], w_proj.shape[1]), x.dtype),
         pltpu.SemaphoreType.DMA((len(shifts),)),
         pltpu.SemaphoreType.DMA((len(shifts),)),
         pltpu.SemaphoreType.DMA,
     ]
-    if following is not None:
-        next_gain, w_bias = following
-        operands += [next_gain[None], jnp.pad(jnp.transpose(w_bias), ((0, 16 - HEADS), (0, 0)))]
+    if turn == 0:
         part_shape = (x.shape[0], HEADS, x.shape[1])
         outs.append(jax.ShapeDtypeStruct((2, size[0] // 2, size[1]) + part_shape, x.dtype))
         count = size[1] - 1 + size[0] // 2
@@ -282,7 +244,7 @@
             pltpu.SemaphoreType.DMA,
         ]
     return pl.pallas_call(
-        functools.partial(fused_kernel, size, shifts, piece_of, place_of, following is not None),
+        functools.partial(fused_kernel, size, shifts, piece_of, place_of, turn),
         out_shape=outs,
         in_specs=[pl.BlockSpec(memory_space=pltpu.VMEM)] * len(operands),
         out_specs=[pl.BlockSpec(memory_space=pltpu.VMEM)] * len(outs),
@@ -307,62 +269,119 @@
     )(part)
 
 
-def gather_bias(x, token_mask, gain, w_bias, size, ending):
+def gather_bias(x, token_mask, gain, w_bias, size):
     rows, count, channels = x.shape
     normed = normalize(x, gain)
     part = jnp.einsum("ikc,ch->ihk", normed, w_bias, preferred_element_type=jnp.float32)
-    full = gather(part.astype(jnp.bfloat16), size, 0 if ending else 1)
-    order = (4, 5, 2, 1, 0, 3) if ending else (4, 5, 1, 0, 2, 3)
-    turned = jnp.transpose(full, order).reshape(HEADS, count, count).astype(jnp.float32) * LOG2E
-    return jnp.where(token_mask[None, :, None] > 0, turned, -1000000000.0)
+    full = gather(part.astype(jnp.bfloat16), size, 1)
+    turned = jnp.transpose(full, (4, 5, 1, 0, 2, 3)).reshape(HEADS, count, count)
+    return finish_bias(turned, token_mask)
+
+
+def finish_bias(turned, token_mask):
+    return jnp.where(token_mask[None, :, None] > 0, turned.astype(jnp.float32) * LOG2E, -1000000000.0)
 
 
 def swap(x, size):
     width, count, channels = x.shape
     rows, cols = size
-    if width % 2:
-        x = lax.all_to_all(x, "row", 1, 0, tiled=True)
-        return lax.all_to_all(jnp.transpose(x, (1, 0, 2)), "col", 0, 1, tiled=True)
-    pairs = width // 2
-    moved = exchange(
-        x.reshape(width, count // 2, 2, channels),
-        (cols, rows, width, pairs, 2, channels),
-        size,
-        ("row", "col"),
-        lambda ref, r, c: ref.at[:, pl.ds((r * cols + c) * pairs, pairs)],
-        lambda ref, r, c: ref.at[c, r],
-        3,
-    )
-    return jnp.transpose(moved.reshape(count, width, channels), (1, 0, 2))
-
-
-def local(pair, token_mask, gain, w_proj, w_bias, w_out, size):
+    x = lax.all_to_all(x, "row", 1, 0, tiled=True)
+    return lax.all_to_all(jnp.transpose(x, (1, 0, 2)), "col", 0, 1, tiled=True)
+
+
+def entry_kernel(
+    size, shifts, piece_of, place_of, pair_ref, flipped_ref, gain_ref, w_bias_ref, x_ref, full_ref, part,
+    send_sems, recv_sems, own_sem, gather_send, gather_recv, gather_own
+):
+    rows, cols = size
+    row, col = lax.axis_index("row"), lax.axis_index("col")
+    to = [(lax.rem(row + dr, rows), col) for dr, dc in shifts]
+    in_col, in_row, partner = gather_peers(size)
+    meet(to + in_col)
+    copies = [
+        remote(piece_of(flipped_ref, *peer), place_of(x_ref, row, col), send_sems.at[at], recv_sems.at[at], peer)
+        for at, peer in enumerate(to)
+    ]
+    for copy in copies:
+        copy.start()
+    own = pltpu.make_async_copy(piece_of(flipped_ref, row, col), place_of(x_ref, row, col), own_sem)
+    own.start()
+
+    def step(at, carry):
+        turned = lax.dot_general(
+            w_bias_ref[0], normalize(pair_ref[at], gain_ref[0:1]), NT, preferred_element_type=jnp.float32
+        )
+        part[at] = turned[:HEADS].astype(jnp.bfloat16)
+        return carry
+
+    lax.fori_loop(0, part.shape[0], step, 0, unroll=4)
+    gather_stages(size, part, full_ref, gather_send, gather_recv, gather_own)
+    own.wait()
+    for at, (dr, dc) in enumerate(shifts):
+        source = lax.rem(row + rows - dr, rows)
+        remote(
+            piece_of(flipped_ref, row, col), place_of(x_ref, source, col), send_sems.at[at], recv_sems.at[at], to[at]
+        ).wait_recv()
+    for copy in copies:
+        copy.wait_send()
+
+
+def entry(pair, gain, w_bias, size):
     rows, cols = size
     deep, wide, channels = pair.shape
     width, count = wide // rows, deep * rows
-    flipped = jnp.transpose(pair, (1, 0, 2))
-    x = exchange(
-        flipped,
-        (width, count, channels),
-        size,
-        ("row",),
-        lambda ref, r, c: ref.at[pl.ds(r * width, width)],
-        lambda ref, r, c: ref.at[:, pl.ds(pl.multiple_of(r * deep, deep), deep)],
-        2,
-    )
-    bias = gather_bias(x, token_mask, gain[0], w_bias[0], size, True)
+    shifts = shifts_of(size, ("row",))
+    part_shape = (deep, HEADS, wide)
+    stages = cols - 1 + rows // 2
+    return pl.pallas_call(
+        functools.partial(
+            entry_kernel,
+            size,
+            shifts,
+            lambda ref, r, c: ref.at[pl.ds(r * width, width)],
+            lambda ref, r, c: ref.at[:, pl.ds(pl.multiple_of(r * deep, deep), deep)],
+        ),
+        out_shape=[
+            jax.ShapeDtypeStruct((width, count, channels), pair.dtype),
+            jax.ShapeDtypeStruct((2, rows // 2, cols) + part_shape, pair.dtype),
+        ],
+        in_specs=[pl.BlockSpec(memory_space=pltpu.VMEM)] * 4,
+        out_specs=[pl.BlockSpec(memory_space=pltpu.VMEM)] * 2,
+        scratch_shapes=[
+            pltpu.VMEM(part_shape, pair.dtype),
+            pltpu.SemaphoreType.DMA((len(shifts),)),
+            pltpu.SemaphoreType.DMA((len(shifts),)),
+            pltpu.SemaphoreType.DMA,
+            pltpu.SemaphoreType.DMA((stages,)),
+            pltpu.SemaphoreType.DMA((stages,)),
+            pltpu.SemaphoreType.DMA,
+        ],
+        compiler_params=pltpu.CompilerParams(collective_id=2, has_side_effects=True),
+    )(pair, jnp.transpose(pair, (1, 0, 2)), gain, w_bias)
+
+
+def local(pair, token_mask, gain, w_proj, w_bias, w_out, size):
+    rows, cols = size
+    deep, wide, channels = pair.shape
+    width, count = wide // rows, deep * rows
+    w_bias_turned = jnp.pad(jnp.transpose(w_bias, (0, 2, 1)), ((0, 0), (0, 16 - HEADS), (0, 0)))
+    x, full = entry(pair, gain, w_bias_turned, size)
+    turned = jnp.transpose(full, (4, 1, 0, 3, 2, 5)).reshape(HEADS, count, count)
+    bias = finish_bias(turned, token_mask)
     if width % 2:
         x = attention(x, bias, gain[0], w_proj[0], w_out[0])
         x = swap(x, size)
-        bias = gather_bias(x, token_mask, gain[1], w_bias[1], size, False)
+        bias = gather_bias(x, token_mask, gain[1], w_bias[1], size)
     else:
         pairs = width // 2
         moved, full = fused(
             x,
             bias,
-            gain[0],
-            w_proj[0],
-            w_out[0],
+            gain,
+            w_proj,
+            w_bias_turned,
+            w_out,
+            0,
             (cols, rows, width, pairs, 2, channels),
             (width, count // 2, 2, channels),
             size,
@@ -370,17 +389,18 @@
             lambda ref, at, r, c: ref.at[at, pl.ds((r * cols + c) * pairs, pairs)],
             lambda ref, at, r, c: ref.at[c, r, at],
             3,
-            (gain[1], w_bias[1]),
         )
         x = jnp.transpose(moved.reshape(count, width, channels), (1, 0, 2))
         turned = jnp.transpose(full, (4, 2, 1, 0, 3, 5)).reshape(HEADS, count, count)
-        bias = jnp.where(token_mask[None, :, None] > 0, turned.astype(jnp.float32) * LOG2E, -1000000000.0)
+        bias = finish_bias(turned, token_mask)
     return fused(
         x,
         bias,
-        gain[1],
-        w_proj[1],
-        w_out[1],
+        gain,
+        w_proj,
+        w_bias_turned,
+        w_out,
+        1,
         pair.shape,
         x.shape,
         size,

time: 164 us -> 144 us (0.88)
  Pallas kernels: 128 us -> 120 us
  other arithmetic: 12.7 us -> 7.98 us
  local copies, waits for them, and re-layouts: 20 us -> 15.5 us
  matrix products: 2.7 us -> 0 us
    pallas_call x2 -> x1, Pallas kernels: 38.9 us -> 33.5 us  [entry(): pl.pallas_call(functools.partial(entry_kernel, size, shifts, lambda ref,...]
    reduce_sum x2 -> x0, other arithmetic: 4.24 us -> none  [the longest x1 2.49 us: normalize(): variance = jnp.mean(centred * centred, axis=-1, keepdims=True)]
    dot_general x1 -> x0, matrix products: 2.7 us -> none  [gather_bias(): jnp.einsum('ikc,ch->ihk', normed, w_bias, preferred_element_type=jnp.floa...]
    slice x7 -> x0, local copies, waits for them, and re-layouts: 2.56 us -> none  [the longest x1 1.29 us: local(): gain[1]]
    squeeze x2 -> x0, local copies, waits for them, and re-layouts: 2.43 us -> none  [the longest x1 1.43 us: local(): w_out[1]]
    pallas_call x2, Pallas kernels: 89.2 us -> 86.9 us  [fused(): pl.pallas_call(functools.partial(fused_kernel, size, shifts, piece_of, pl...]
    unnamed x10 -> x8, local copies, waits for them, and re-layouts: 3.85 us -> 5.13 us
where the time goes in v2:
time: 144 us
  Pallas kernels  120 us (83%)
  local copies, waits for them, and re-layouts  15.5 us (11%)
  other arithmetic  7.98 us (6%)
    pallas_call x2, Pallas kernels, fused(): pl.pallas_call(functools.partial(fused_kernel, size, shifts, piece_of, pl...  86.9 us
    pallas_call x1, Pallas kernels, entry(): pl.pallas_call(functools.partial(entry_kernel, size, shifts, lambda ref,...  33.5 us
    mul x3, local copies, waits for them, and re-layouts, finish_bias(): turned.astype(jnp.float32) * LOG2E  5.25 us
    unnamed x8, local copies, waits for them, and re-layouts  5.13 us
    select_n x2, other arithmetic, finish_bias(): jnp.where(token_mask[None, :, None] > 0, turned.astype(jnp.float32) * LOG...  5.1 us
    reshape x2, local copies, waits for them, and re-layouts, local(): x = jnp.transpose(moved.reshape(count, width, channels), (1, 0, 2))  4.53 us

profile of v2, /device:TPU:0, one launch (start us, length us, event | category | flops | bytes accessed | tf_op | source)
XLA Modules:
  0.0 144.0 jit_solution(12793583008874490288)
XLA Ops:
  0.0 0.0 copy-start.2
  0.0 2.8 %copy.21 = bf16[48,96,128]{2,0,1:T(8,128)(2,1)} copy(bf16[48,96,128]{2,1,0:T(8,128)(2,1)} %pair_ref.1) | data formatting | bytes 2359296 | tf_op args[0]
  2.8 0.0 copy-done.2
  2.8 0.6 pad.4.w_bias_ref
  3.3 33.5 %shard_map.64 = (bf16[12,384,128]{2,1,0:T(8,128)(2,1)}, bf16[2,4,4,48,4,96]{5,4,3,2,1,0:T(4,128)(2,1)}) custom-call(bf16[48,96,128]{2,1,0:T(8,128)(2,1)} %pair_ref.1, bf16[96,48,128]{2,1,0:T(8,128)(2,1)} %bitcast.13, f32[2,128]{1,0:T(2,128)} %gain_ref.5, bf16[2,16,128]{2,1,0:T(8,128)(2,1)} %pad.4.w_bias_ref), custom_call_target="tpu_custom_call" | custom-call | tf_op jit(solution)/shard_map/pallas_call | solution.py:336
  36.8 2.3 %multiply_bitcast_fusion = f32[4,4,2,48,4,96]{5,0,3,4,1,2:T(4,128)S(1)} fusion(bf16[2,4,4,48,4,96]{5,4,3,2,1,0:T(4,128)(2,1)} %get-tuple-element.10), kind=kLoop, calls=%fused_computation | loop fusion | flops 1179648 | bytes 3538944 | tf_op jit(solution)/shard_map/mul | solution.py:282
  39.1 2.0 %copy.12 = f32[4,4,2,48,4,96]{5,4,3,2,1,0:T(4,128)S(1)} copy(f32[4,4,2,48,4,96]{5,0,3,4,1,2:T(4,128)S(1)} %multiply_bitcast_fusion) | data formatting | bytes 4718592 | tf_op jit(solution)/shard_map/mul | solution.py:282
  41.1 0.0 copy-start.1
  41.1 2.6 %mul.20 = f32[4,384,384]{2,1,0:T(8,128)} reshape(f32[4,4,2,48,4,96]{5,4,3,2,1,0:T(4,128)S(1)} %copy.12) | data formatting | bytes 4718592 | tf_op jit(solution)/shard_map/mul | solution.py:282
  43.8 0.0 copy-done.1
  43.8 3.4 %broadcast_select_fusion.bias_ref = f32[4,384,384]{2,1,0:T(8,128)} fusion(f32[4,384,384]{2,1,0:T(8,128)} %mul.20, pred[384]{0:T(512)(128)(4,1)S(1)} %broadcast_compare_fusion), kind=kLoop, calls=%fused_computation.5 | loop fusion | flops 589824 | bytes 4718976 | tf_op jit(solution)/shard_map/jit(_where)/select_n | solution.py:282
  47.1 51.8 %shard_map.65 = (bf16[4,8,12,6,2,128]{5,4,3,2,1,0:T(2,128)(2,1)}, bf16[2,4,4,12,4,384]{5,4,3,2,1,0:T(4,128)(2,1)}) custom-call(bf16[12,384,128]{2,1,0:T(8,128)(2,1)} %get-tuple-element.9.x_ref, f32[4,384,384]{2,1,0:T(8,128)} %broadcast_select_fusion.bias_ref, f32[2,128]{1,0:T(2,128)} %gain_ref.5, bf16[2,128,512]{2,1,0:T(8,128)(2,1)} %w_proj_ref.3, ...), custom_call_target="tpu_custom_call" | custom-call | tf_op jit(solution)/shard_map/pallas_call | solution.py:246
  99.0 0.0 copy-start
  99.0 3.2 %reshape.14 = bf16[384,12,128]{2,1,0:T(8,128)(2,1)S(1)} reshape(bf16[4,8,12,6,2,128]{5,4,3,2,1,0:T(2,128)(2,1)} %get-tuple-element.11) | data formatting | bytes 2359296 | tf_op jit(solution)/shard_map/reshape | solution.py:393
  102.2 1.3 copy.20
  103.5 0.0 copy-done
  103.5 0.6 multiply_bitcast_fusion.1
  104.2 0.6 copy.14
  104.8 1.7 %copy_select_fusion.bias_ref = f32[4,384,384]{2,1,0:T(8,128)} fusion(f32[4,384,384]{2,0,1:T(4,128)S(1)} %bitcast.12, pred[384]{0:T(512)(128)(4,1)S(1)} %broadcast_compare_fusion), kind=kLoop, calls=%fused_computation.1 | loop fusion | flops 589824 | bytes 4718976 | tf_op jit(solution)/shard_map/jit(_where)/select_n | solution.py:282
  106.5 35.1 %shard_map.66 = bf16[48,96,128]{2,1,0:T(8,128)(2,1)} custom-call(bf16[12,384,128]{2,1,0:T(8,128)(2,1)} %bitcast.14, f32[4,384,384]{2,1,0:T(8,128)} %copy_select_fusion.bias_ref, f32[2,128]{1,0:T(2,128)} %gain_ref.5, bf16[2,128,512]{2,1,0:T(8,128)(2,1)} %w_proj_ref.3, bf16[2,16,128]{2,1,0:T(8,128)(2,1)} %pad.4.w_bias_ref, bf16[2,128,128]{2,1,0:T(8,128)(2,1)} %w_out_ref.3), custom_call_target="tpu_custom_call" | custom-call | tf_op jit(solution)/shard_map/pallas_call | solution.py:246
  141.6 2.4 %copy.23 = bf16[48,96,128]{2,1,0:T(8,128)(2,1)} copy(bf16[48,96,128]{2,1,0:T(8,128)(2,1)} %shard_map.66) | data formatting | bytes 2359296
  (1 shorter events, 0.0 us)
Async XLA Ops:
  0.0 2.8 %copy-start.2 = (bf16[2,128,4]{1,2,0:T(4,128)(2,1)S(1)}, bf16[2,128,4]{1,2,0:T(4,128)(2,1)}, u32[]{:S(2)}) copy-start(bf16[2,128,4]{1,2,0:T(4,128)(2,1)} %param.10) | copy-start | bytes 6148
  41.1 2.6 %copy-start.1 = (s32[384]{0:T(512)S(1)}, s32[384]{0:T(512)}, u32[]{:S(2)}) copy-start(s32[384]{0:T(512)} %param.7) | copy-start | bytes 4612
  99.0 4.6 %copy-start = (bf16[2,4,4,12,4,384]{5,4,3,2,1,0:T(4,128)(2,1)S(1)}, bf16[2,4,4,12,4,384]{5,4,3,2,1,0:T(4,128)(2,1)}, u32[]{:S(2)}) copy-start(bf16[2,4,4,12,4,384]{5,4,3,2,1,0:T(4,128)(2,1)} %get-tuple-element.12) | copy-start | bytes 3538948

commit v3 on v2

--- a/solution.py
+++ b/solution.py
@@ -12,6 +12,7 @@
 HEAD_DIM = 32
 INNER = HEADS * HEAD_DIM
 LOG2E = 1.4426950408889634
+LAG = 2
 NT = (((1,), (1,)), ((), ()))
 TN = (((0,), (0,)), ((), ()))
 
@@ -104,7 +105,7 @@
     return in_col, in_row, partner
 
 
-def gather_stages(size, part_ref, full_ref, send_sems, recv_sems, own_sem):
+def gather_stages(size, part_ref, full_ref, send_sems, recv_sems, own_sem, between=()):
     rows, cols = size
     row, col = lax.axis_index("row"), lax.axis_index("col")
     half, core = row // 2, lax.rem(row, 2)
@@ -130,6 +131,8 @@
     base = len(in_col)
     for at, peer in enumerate(in_row):
         send(full_ref.at[core, half], full_ref.at[core, half], base + at, peer)
+    for copy in between:
+        copy.start()
     halves = rows // 2
     for at, peer in enumerate(in_row):
         arrive(full_ref.at[core, lax.rem(half + halves - at - 1, halves)], base + at, peer)
@@ -146,15 +149,83 @@
     gather_stages(size, part_ref, full_ref, send_sems, recv_sems, own_sem)
 
 
+def gather_steps(size, part, full_ref, send_sems, recv_sems, own_sems):
+    rows, cols = size
+    row, col = lax.axis_index("row"), lax.axis_index("col")
+    half, core, halves = row // 2, lax.rem(row, 2), rows // 2
+    in_col, in_row, partner = gather_peers(size)
+    base = len(in_col)
+    last = base + len(in_row)
+
+    def link(source, target, at, index, peer):
+        return remote(source, target, send_sems.at[at, index], recv_sems.at[at, index], peer)
+
+    def own(at):
+        return pltpu.make_async_copy(part.at[at], full_ref.at[core, half, col, at], own_sems.at[at])
+
+    def to_col(at):
+        mine = full_ref.at[core, half, col, at]
+        return [link(part.at[at], mine, at, index, peer) for index, peer in enumerate(in_col)]
+
+    def to_row(at):
+        line = full_ref.at[core, half, :, at]
+        return [link(line, line, at, base + index, peer) for index, peer in enumerate(in_row)]
+
+    def to_partner(at):
+        plane = full_ref.at[core, :, :, at]
+        return link(plane, plane, at, last, partner)
+
+    def send_part(at):
+        own(at).start()
+        for copy in to_col(at):
+            copy.start()
+
+    def pass_on(at):
+        own(at).wait()
+        for index, peer in enumerate(in_col):
+            place = full_ref.at[core, half, lax.rem(col + cols - index - 1, cols), at]
+            link(place, place, at, index, peer).wait_recv()
+        for copy in to_row(at):
+            copy.start()
+
+    def share(at):
+        for index, peer in enumerate(in_row):
+            line = full_ref.at[core, lax.rem(half + halves - index - 1, halves), :, at]
+            link(line, line, at, base + index, peer).wait_recv()
+        to_partner(at).start()
+
+    def finish(at, carry):
+        plane = full_ref.at[1 - core, :, :, at]
+        link(plane, plane, at, last, partner).wait_recv()
+        for copy in to_col(at) + to_row(at) + [to_partner(at)]:
+            copy.wait_send()
+        return carry
+
+    return send_part, pass_on, share, finish
+
+
+def assemble(first_ref, mask_ref, bias_ref):
+    cores, halves, cols, heads, deep, wide = first_ref.shape
+    for half in range(halves):
+        for core in range(cores):
+            place = pl.ds((half * cores + core) * deep, deep)
+            live = mask_ref[place] > 0
+            for head in range(heads):
+                pieces = [first_ref[core, half, col, head].astype(jnp.float32) for col in range(cols)]
+                block = jnp.concatenate(pieces, axis=1) * LOG2E
+                bias_ref[head, place, :] = jnp.where(live, block, -1000000000.0)
+
+
 def fused_kernel(
-    size, shifts, piece_of, place_of, turn, x_ref, bias_ref, gain_ref, w_proj_ref, w_bias_ref, w_out_ref, *rest
+    size, shifts, piece_of, place_of, turn, x_ref, gain_ref, w_proj_ref, w_bias_ref, w_out_ref, *rest
 ):
     bias_too = turn == 0
+    group = 2 if bias_too else 1
     if bias_too:
-        out_ref, full_ref, stage, turned_ref, send_sems, recv_sems, own_sem = rest[:7]
-        part, gather_send, gather_recv, gather_own = rest[7:]
+        first_ref, mask_ref, out_ref, full_ref, stage, turned_ref, send_sems, recv_sems, own_sem = rest[:9]
+        bias_ref, part, gather_send, gather_recv, gather_own = rest[9:]
     else:
-        out_ref, stage, turned_ref, send_sems, recv_sems, own_sem = rest
+        bias_ref, out_ref, stage, turned_ref, send_sems, recv_sems, own_sem = rest
     width = x_ref.shape[0]
     rows, cols = size
     row, col = lax.axis_index("row"), lax.axis_index("col")
@@ -163,7 +234,7 @@
     turned_ref[...] = jnp.transpose(w_proj_ref[turn].astype(jnp.float32)).astype(jnp.bfloat16)
 
     def push(at):
-        one = pl.ds(at, 1)
+        one = pl.ds(at, group)
         for index, peer in enumerate(to):
             remote(
                 piece_of(stage, one, *peer),
@@ -174,11 +245,11 @@
             ).start()
         pltpu.make_async_copy(piece_of(stage, one, row, col), place_of(out_ref, one, row, col), own_sem).start()
 
-    def step(at, carry):
-        @pl.when(at > 0)
-        def _():
-            push(at - 1)
-
+    if bias_too:
+        assemble(first_ref, mask_ref, bias_ref)
+        send_part, pass_on, share, finish = gather_steps(size, part, full_ref, gather_send, gather_recv, gather_own)
+
+    def compute(at):
         result = attend(
             x_ref[at],
             bias_ref,
@@ -193,12 +264,30 @@
                 w_bias_ref[1], normalize(result, gain_ref[1:2]), NT, preferred_element_type=jnp.float32
             )
             part[at] = turned[:HEADS].astype(jnp.bfloat16)
+
+    def step(at, carry):
+        actions = []
+        if bias_too:
+            actions = [(1, send_part), (1 + LAG, pass_on), (1 + 2 * LAG, share)]
+        @pl.when((at >= group) & (at <= width) & (lax.rem(at, group) == 0))
+        def _():
+            push(at - group)
+
+        for delay, action in actions:
+
+            @pl.when((at >= delay) & (at < width + delay))
+            def _():
+                action(at - delay)
+
+        @pl.when(at < width)
+        def _():
+            compute(at)
+
         return carry
 
-    lax.fori_loop(0, width, step, 0)
-    push(width - 1)
+    lax.fori_loop(0, width + 1 + (2 * LAG if bias_too else 0), step, 0)
     if bias_too:
-        gather_stages(size, part, full_ref, gather_send, gather_recv, gather_own)
+        lax.fori_loop(0, width, finish, 0)
     every = pl.ds(0, width)
     mine = piece_of(stage, every, row, col)
     pltpu.make_async_copy(mine, place_of(out_ref, every, row, col), own_sem).wait()
@@ -224,7 +313,7 @@
 
 def fused(x, bias, gain, w_proj, w_bias, w_out, turn, out_shape, stage_shape, size, axes, piece_of, place_of, collective_id):
     shifts = shifts_of(size, axes)
-    operands = [x, bias, gain, w_proj, w_bias, w_out]
+    operands = [x, gain, w_proj, w_bias, w_out, *bias]
     outs = [jax.ShapeDtypeStruct(out_shape, x.dtype)]
     scratch = [
         pltpu.VMEM(stage_shape, x.dtype),
@@ -238,10 +327,11 @@
         outs.append(jax.ShapeDtypeStruct((2, size[0] // 2, size[1]) + part_shape, x.dtype))
         count = size[1] - 1 + size[0] // 2
         scratch += [
+            pltpu.VMEM((HEADS, x.shape[1], x.shape[1]), jnp.float32),
             pltpu.VMEM(part_shape, x.dtype),
-            pltpu.SemaphoreType.DMA((count,)),
-            pltpu.SemaphoreType.DMA((count,)),
-            pltpu.SemaphoreType.DMA,
+            pltpu.SemaphoreType.DMA((x.shape[0], count)),
+            pltpu.SemaphoreType.DMA((x.shape[0], count)),
+            pltpu.SemaphoreType.DMA((x.shape[0],)),
         ]
     return pl.pallas_call(
         functools.partial(fused_kernel, size, shifts, piece_of, place_of, turn),
@@ -290,7 +380,7 @@
 
 
 def entry_kernel(
-    size, shifts, piece_of, place_of, pair_ref, flipped_ref, gain_ref, w_bias_ref, x_ref, full_ref, part,
+    size, shifts, piece_of, place_of, pair_ref, flipped_ref, gain_ref, w_bias_ref, x_ref, full_ref, part, wide_part,
     send_sems, recv_sems, own_sem, gather_send, gather_recv, gather_own
 ):
     rows, cols = size
@@ -302,7 +392,8 @@
         remote(piece_of(flipped_ref, *peer), place_of(x_ref, row, col), send_sems.at[at], recv_sems.at[at], peer)
         for at, peer in enumerate(to)
     ]
-    for copy in copies:
+    early = len(copies) // 2
+    for copy in copies[:early]:
         copy.start()
     own = pltpu.make_async_copy(piece_of(flipped_ref, row, col), place_of(x_ref, row, col), own_sem)
     own.start()
@@ -311,11 +402,13 @@
         turned = lax.dot_general(
             w_bias_ref[0], normalize(pair_ref[at], gain_ref[0:1]), NT, preferred_element_type=jnp.float32
         )
-        part[at] = turned[:HEADS].astype(jnp.bfloat16)
+        wide_part[at] = turned[:HEADS]
         return carry
 
-    lax.fori_loop(0, part.shape[0], step, 0, unroll=4)
-    gather_stages(size, part, full_ref, gather_send, gather_recv, gather_own)
+    lax.fori_loop(0, pair_ref.shape[0], step, 0, unroll=4)
+    for head in range(HEADS):
+        part[head] = wide_part[:, head, :].astype(jnp.bfloat16)
+    gather_stages(size, part, full_ref, gather_send, gather_recv, gather_own, copies[early:])
     own.wait()
     for at, (dr, dc) in enumerate(shifts):
         source = lax.rem(row + rows - dr, rows)
@@ -331,7 +424,7 @@
     deep, wide, channels = pair.shape
     width, count = wide // rows, deep * rows
     shifts = shifts_of(size, ("row",))
-    part_shape = (deep, HEADS, wide)
+    part_shape = (HEADS, deep, wide)
     stages = cols - 1 + rows // 2
     return pl.pallas_call(
         functools.partial(
@@ -349,6 +442,7 @@
         out_specs=[pl.BlockSpec(memory_space=pltpu.VMEM)] * 2,
         scratch_shapes=[
             pltpu.VMEM(part_shape, pair.dtype),
+            pltpu.VMEM((deep, HEADS, wide), jnp.float32),
             pltpu.SemaphoreType.DMA((len(shifts),)),
             pltpu.SemaphoreType.DMA((len(shifts),)),
             pltpu.SemaphoreType.DMA,
@@ -366,9 +460,9 @@
     width, count = wide // rows, deep * rows
     w_bias_turned = jnp.pad(jnp.transpose(w_bias, (0, 2, 1)), ((0, 0), (0, 16 - HEADS), (0, 0)))
     x, full = entry(pair, gain, w_bias_turned, size)
-    turned = jnp.transpose(full, (4, 1, 0, 3, 2, 5)).reshape(HEADS, count, count)
-    bias = finish_bias(turned, token_mask)
     if width % 2:
+        turned = jnp.transpose(full, (3, 1, 0, 4, 2, 5)).reshape(HEADS, count, count)
+        bias = finish_bias(turned, token_mask)
         x = attention(x, bias, gain[0], w_proj[0], w_out[0])
         x = swap(x, size)
         bias = gather_bias(x, token_mask, gain[1], w_bias[1], size)
@@ -376,7 +470,7 @@
         pairs = width // 2
         moved, full = fused(
             x,
-            bias,
+            (full, token_mask.reshape(count, 1)),
             gain,
             w_proj,
             w_bias_turned,
@@ -395,7 +489,7 @@
         bias = finish_bias(turned, token_mask)
     return fused(
         x,
-        bias,
+        (bias,),
         gain,
         w_proj,
         w_bias_turned,

time: 144 us -> 138 us (0.958)
  other arithmetic: 7.98 us -> 3.05 us
  local copies, waits for them, and re-layouts: 15.5 us -> 12.9 us
  Pallas kernels: 120 us -> 122 us
    mul x3 -> x1, local copies, waits for them, and re-layouts: 5.25 us -> 0.61 us  [finish_bias(): turned.astype(jnp.float32) * LOG2E]
    select_n x2 -> x1, other arithmetic: 5.1 us -> 1.74 us  [finish_bias(): jnp.where(token_mask[None, :, None] > 0, turned.astype(jnp.float32) * LOG...]
    pallas_call x2, Pallas kernels: 86.9 us -> 90.2 us  [fused(): pl.pallas_call(functools.partial(fused_kernel, size, shifts, piece_of, pl...]
    mul x2 -> x1, other arithmetic: 2.88 us -> 0.62 us  [finish_bias(): turned.astype(jnp.float32) * LOG2E]
    pallas_call x1, Pallas kernels: 33.5 us -> 31.7 us  [entry(): pl.pallas_call(functools.partial(entry_kernel, size, shifts, lambda ref,...]
    reshape x0 -> x1, local copies, waits for them, and re-layouts: none -> 1.48 us  [local(): token_mask.reshape(count, 1)]
    unnamed x8 -> x4, local copies, waits for them, and re-layouts: 5.13 us -> 5.1 us
where the time goes in v3:
time: 138 us
  Pallas kernels  122 us (88%)
  local copies, waits for them, and re-layouts  12.9 us (9%)
  other arithmetic  3.05 us (2%)
    pallas_call x2, Pallas kernels, fused(): pl.pallas_call(functools.partial(fused_kernel, size, shifts, piece_of, pl...  90.2 us
    pallas_call x1, Pallas kernels, entry(): pl.pallas_call(functools.partial(entry_kernel, size, shifts, lambda ref,...  31.7 us
    unnamed x4, local copies, waits for them, and re-layouts  5.1 us
    reshape x2, local copies, waits for them, and re-layouts, local(): x = jnp.transpose(moved.reshape(count, width, channels), (1, 0, 2))  4.44 us

profile of v3, /device:TPU:0, one launch (start us, length us, event | category | flops | bytes accessed | tf_op | source)
XLA Modules:
  0.0 137.9 jit_solution(18020752823597321820)
XLA Ops:
  0.0 0.7 broadcast_compare_fusion
  0.7 1.3 pad.4.w_bias_ref
  2.0 1.5 %reshape.14.rest_1_ = s32[384,1]{1,0:T(8,128)} reshape(s32[384]{0:T(512)} %param.7) | data formatting | bytes 3072 | tf_op jit(solution)/shard_map/reshape | solution.py:473
  3.5 2.7 %copy.20 = bf16[48,96,128]{2,0,1:T(8,128)(2,1)} copy(bf16[48,96,128]{2,1,0:T(8,128)(2,1)} %pair_ref.1) | data formatting | bytes 2359296 | tf_op args[0]
  6.2 31.7 %shard_map.64 = (bf16[12,384,128]{2,1,0:T(8,128)(2,1)}, bf16[2,4,4,4,48,96]{5,4,3,2,1,0:T(8,128)(2,1)}) custom-call(bf16[48,96,128]{2,1,0:T(8,128)(2,1)} %pair_ref.1, bf16[96,48,128]{2,1,0:T(8,128)(2,1)} %bitcast.11, f32[2,128]{1,0:T(2,128)} %gain_ref.5, bf16[2,16,128]{2,1,0:T(8,128)(2,1)} %pad.4.w_bias_ref), custom_call_target="tpu_custom_call" | custom-call | tf_op jit(solution)/shard_map/pallas_call | solution.py:429
  37.9 55.9 %shard_map.65 = (bf16[4,8,12,6,2,128]{5,4,3,2,1,0:T(2,128)(2,1)}, bf16[2,4,4,12,4,384]{5,4,3,2,1,0:T(4,128)(2,1)}) custom-call(bf16[12,384,128]{2,1,0:T(8,128)(2,1)} %get-tuple-element.9.x_ref, f32[2,128]{1,0:T(2,128)} %gain_ref.5, bf16[2,128,512]{2,1,0:T(8,128)(2,1)} %w_proj_ref.3, bf16[2,16,128]{2,1,0:T(8,128)(2,1)} %pad.4.w_bias_ref, ...), custom_call_target="tpu_custom_call" | custom-call | tf_op jit(solution)/shard_map/pallas_call | solution.py:336
  93.8 3.1 %reshape.15 = bf16[384,12,128]{2,1,0:T(8,128)(2,1)S(1)} reshape(bf16[4,8,12,6,2,128]{5,4,3,2,1,0:T(2,128)(2,1)} %get-tuple-element.11) | data formatting | bytes 2359296 | tf_op jit(solution)/shard_map/reshape | solution.py:487
  96.9 0.0 copy-start
  96.9 1.3 copy.19
  98.3 0.0 copy-done
  98.3 0.6 multiply_bitcast_fusion
  98.9 0.6 copy.13
  99.5 1.7 %copy_select_fusion.rest_0_ = f32[4,384,384]{2,1,0:T(8,128)} fusion(f32[4,384,384]{2,0,1:T(4,128)S(1)} %bitcast.10, pred[384]{0:T(512)(128)(4,1)S(1)} %broadcast_compare_fusion), kind=kLoop, calls=%fused_computation | loop fusion | flops 589824 | bytes 4718976 | tf_op jit(solution)/shard_map/jit(_where)/select_n | solution.py:372
  101.3 34.3 %shard_map.66 = bf16[48,96,128]{2,1,0:T(8,128)(2,1)} custom-call(bf16[12,384,128]{2,1,0:T(8,128)(2,1)} %bitcast.12, f32[2,128]{1,0:T(2,128)} %gain_ref.5, bf16[2,128,512]{2,1,0:T(8,128)(2,1)} %w_proj_ref.3, bf16[2,16,128]{2,1,0:T(8,128)(2,1)} %pad.4.w_bias_ref, bf16[2,128,128]{2,1,0:T(8,128)(2,1)} %w_out_ref.3, f32[4,384,384]{2,1,0:T(8,128)} %copy_select_fusion.rest_0_), custom_call_target="tpu_custom_call" | custom-call | tf_op jit(solution)/shard_map/pallas_call | solution.py:336
  135.6 2.4 %copy.22 = bf16[48,96,128]{2,1,0:T(8,128)(2,1)} copy(bf16[48,96,128]{2,1,0:T(8,128)(2,1)} %shard_map.66) | data formatting | bytes 2359296
Async XLA Ops:
  96.9 1.3 copy-start
